TPU v7x, 32 devices: a whole 2x2x4 slice. The times are simulated.
32 devices in a mesh: dp: 8 (over y, x, core), tensor: 4 (over z).
Axes of the slice: x: 2, y: 2, z: 4, core: 2. Of those that a mesh axis runs over, the one named last changes fastest.
Arguments:
- hidden_in: bfloat16 [16384, 768], P(('dp', 'tensor')), may hold values from -6 to 6
- token_types: int32 [16384], P('dp'), may hold values 0 or 1
- lengths: int32 [8], P('dp'), may hold values from 512 to 2048, as said below
- cotangent: bfloat16 [16384, 768], P(('dp', 'tensor')), may hold values from -6 to 6
- query_w: bfloat16 [4, 768, 768], P(None, 'dp', 'tensor'), may hold values from -0.4375 to 0.4375
- query_b: bfloat16 [4, 768], replicated, may hold values from -3 to 3
- key_w: bfloat16 [768, 768], P('dp', 'tensor'), may hold values from -0.21875 to 0.21875
- value_w: bfloat16 [768, 768], P('dp', 'tensor'), may hold values from -0.21875 to 0.21875
- value_b: bfloat16 [768], replicated, may hold values from -3 to 3
- out_w: bfloat16 [768, 768], P('tensor', 'dp'), may hold values from -0.875 to 0.875
- out_b: bfloat16 [768], replicated, may hold values from -3 to 3
- gain_one: bfloat16 [768], replicated, may hold values from 0.099609375 to 1.8984375
- shift_one: bfloat16 [768], replicated, may hold values from -3 to 3
- inter_w: bfloat16 [768, 3072], P('dp', 'tensor'), may hold values from -0.21875 to 0.21875
- inter_b: bfloat16 [3072], replicated, may hold values from -3 to 3
- output_w: bfloat16 [3072, 768], P('tensor', 'dp'), may hold values from -0.109375 to 0.109375
- output_b: bfloat16 [768], replicated, may hold values from -3 to 3
- gain_two: bfloat16 [768], replicated, may hold values from 0.099609375 to 1.8984375
- shift_two: bfloat16 [768], replicated, may hold values from -3 to 3
Outputs:
- layer_out: bfloat16 [16384, 768], P(('dp', 'tensor'))
- grad_hidden: float32 [16384, 768], P(('dp', 'tensor'))
- query_weight_gradient: float32 [4, 768, 768], P(None, 'dp', 'tensor')
- grad_query_b: float32 [4, 768], replicated
- grad_key_w: float32 [768, 768], P('dp', 'tensor')
- grad_value_w: float32 [768, 768], P('dp', 'tensor')
- grad_value_b: float32 [768], replicated
- grad_out_w: float32 [768, 768], P('tensor', 'dp')
- grad_out_b: float32 [768], replicated
- grad_gain_one: float32 [768], replicated
- grad_shift_one: float32 [768], replicated
- grad_inter_w: float32 [768, 3072], P('dp', 'tensor')
- grad_inter_b: float32 [3072], replicated
- grad_output_w: float32 [3072, 768], P('tensor', 'dp')
- grad_output_b: float32 [768], replicated
- grad_gain_two: float32 [768], replicated
- grad_shift_two: float32 [768], replicated
Inputs may be any that keep to these rules, and one draw needn't show every extreme that they name: `lengths`: valid slots of each sequence; in every draw one sequence is full and another has exactly 512 valid slots.
All inputs are finite; a program needn't handle non-finite values. No bound on the sum of `token_types` on one device may be relied on, other than what follows from the above.
Results may differ from a plain program's by a relative error of at most 0.019.
The roundings to bfloat16 on the way count: a program that leaves them out, or rounds other values in their place, can miss the bound.
Values may be sent and summed in bfloat16 or wider, within the bound.
No kernel may reach another device: no remote copies, remote signals or barrier semaphores. Data moves between devices by JAX's collectives and lax.ppermute only.
A program may use at most 192 MiB of HBM per device.

v0:
```python
import jax
import jax.numpy as jnp
from jax import lax
from jax.sharding import PartitionSpec as P

HD = 64
BLOCK = 512


def in_blocks(value, dim, peers):
    before, after = (value.shape[:dim], value.shape[dim + 1 :])
    return jnp.moveaxis(value.reshape(*before, peers, -1, *after), dim, 0)


def summed_on_arrival(value, axis, dim):
    blocks = in_blocks(value, dim, lax.axis_size(axis))
    arrived = lax.all_to_all(blocks, axis, split_axis=0, concat_axis=0, tiled=True)
    return arrived.astype(jnp.float32).sum(axis=0)


def side_by_side(arrays, axis, dim, along):
    both = jnp.concatenate(arrays, axis=along)
    result, at, finished = (summed_on_arrival(both, axis, dim), 0, [])
    for a in arrays:
        finished.append(lax.slice_in_dim(result, at, at + a.shape[along], axis=along))
        at += a.shape[along]
    return tuple(finished)


def layer_norm(residual, norm_gain, norm_shift):
    center = residual - jnp.mean(residual, -1, keepdims=True)
    spread = jnp.mean(center * center, -1, keepdims=True)
    return center * lax.rsqrt(spread + 1e-05) * norm_gain + norm_shift


def exact_gelu(values_in):
    return jax.nn.gelu(values_in, approximate=False)


def local(
    hidden_in,
    token_types,
    lengths,
    cotangent,
    query_w,
    query_b,
    key_w,
    value_w,
    value_b,
    out_w,
    out_b,
    gain_one,
    shift_one,
    inter_w,
    inter_b,
    output_w,
    output_b,
    gain_two,
    shift_two,
):
    single_float = jnp.float32
    bf16 = jnp.bfloat16
    groups = lax.axis_size("tensor")
    member = lax.axis_index("tensor")
    own_rows = hidden_in.shape[0]
    width_full = hidden_in.shape[1]
    length = own_rows * groups
    width_group = query_w.shape[2]
    heads_group = width_group // HD
    ffn_group = inter_w.shape[1]
    blocks = length // BLOCK
    score_scale = HD ** (-0.5)
    positions = jnp.arange(length, dtype=jnp.int32)
    valid_all = (positions < lengths[0]).astype(single_float)
    valid_own = lax.dynamic_slice_in_dim(valid_all, member * own_rows, own_rows)
    entity = token_types.astype(single_float)
    word_flag = 1.0 - entity
    entity_low = entity.astype(bf16)
    word_low = word_flag.astype(bf16)
    col_start = member * width_group
    unit_start = member * ffn_group
    query_b_own = lax.dynamic_slice_in_dim(query_b, col_start, width_group, 1).astype(single_float)
    value_b_own = lax.dynamic_slice_in_dim(value_b, col_start, width_group).astype(single_float)
    inter_b_own = lax.dynamic_slice_in_dim(inter_b, unit_start, ffn_group).astype(single_float)
    query_complete, key_full, value_full, out_full, inter_full, output_full = (
        lax.all_gather(query_w, "dp", axis=1, tiled=True),
        lax.all_gather(key_w, "dp", axis=0, tiled=True),
        lax.all_gather(value_w, "dp", axis=0, tiled=True),
        lax.all_gather(out_w, "dp", axis=1, tiled=True),
        lax.all_gather(inter_w, "dp", axis=0, tiled=True),
        lax.all_gather(output_w, "dp", axis=1, tiled=True),
    )

    def head_major(matrix):
        return matrix.reshape(length, heads_group, HD).transpose(1, 0, 2)

    def token_major(stacked):
        return stacked.transpose(1, 0, 2).reshape(length, width_group)

    complete_input = lax.all_gather(hidden_in, "tensor", axis=0, tiled=True)
    query_all = (
        jnp.einsum(
            "be,qeg->bqg", complete_input, query_complete, preferred_element_type=single_float
        )
        + query_b_own[None]
    )
    entity_side = entity[:, None] > 0.5
    to_word = jnp.where(entity_side, query_all[:, 2], query_all[:, 0])
    to_entity = jnp.where(entity_side, query_all[:, 3], query_all[:, 1])
    query_cat = jnp.concatenate([head_major(to_word), head_major(to_entity)], -1).astype(bf16)
    key_rows = jnp.dot(complete_input, key_full, preferred_element_type=single_float).astype(bf16)
    key_heads = head_major(key_rows)
    key_cat = jnp.concatenate(
        [key_heads * word_low[None, :, None], key_heads * entity_low[None, :, None]], -1
    )
    values = (
        jnp.dot(complete_input, value_full, preferred_element_type=single_float) + value_b_own
    ).astype(bf16)
    value_heads = head_major(values)

    def block_parts(step_index):
        head_index = step_index // blocks
        row_start = step_index % blocks * BLOCK
        query_head = lax.dynamic_index_in_dim(query_cat, head_index, 0, keepdims=False)
        query_block = lax.dynamic_slice_in_dim(query_head, row_start, BLOCK, 0)
        key_head = lax.dynamic_index_in_dim(key_cat, head_index, 0, keepdims=False)
        value_head = lax.dynamic_index_in_dim(value_heads, head_index, 0, keepdims=False)
        raw_scores = (
            jnp.einsum("qc,kc->qk", query_block, key_head, preferred_element_type=single_float)
            * score_scale
        )
        masked = jnp.where(valid_all[None, :] > 0.5, raw_scores, -1e30)
        return (head_index, row_start, query_block, key_head, value_head, masked)

    def attend(step_index):
        head_index, row_start, query_block, key_head, value_head, masked = block_parts(step_index)
        row_max = jnp.max(masked, -1, keepdims=True)
        exponent = jnp.exp(masked - row_max)
        row_total = jnp.sum(exponent, -1, keepdims=True)
        attn_probs = (exponent / row_total).astype(bf16)
        mixed_block = jnp.dot(attn_probs, value_head, preferred_element_type=single_float).astype(
            bf16
        )
        return (mixed_block, (row_max + jnp.log(row_total))[:, 0])

    mixed_all, log_norm = lax.map(attend, jnp.arange(heads_group * blocks))
    mixed_flat = token_major(mixed_all.reshape(heads_group, length, HD))
    attn_part = jnp.dot(mixed_flat, out_full, preferred_element_type=single_float)
    attended = lax.psum_scatter(
        attn_part.astype(jnp.bfloat16), "tensor", scatter_dimension=0, tiled=True
    ).astype(jnp.float32) + out_b.astype(single_float)
    resid_one = hidden_in.astype(single_float) + attended
    normed_one, norm_one_back = jax.vjp(
        layer_norm, resid_one, gain_one.astype(single_float), shift_one.astype(single_float)
    )
    full_normed = lax.all_gather(normed_one.astype(bf16), "tensor", axis=0, tiled=True)
    inner_pre = jnp.dot(full_normed, inter_full, preferred_element_type=single_float) + inter_b_own
    active_f, gelu_back = jax.vjp(exact_gelu, inner_pre)
    active = active_f.astype(bf16)
    unit_part = jnp.dot(active, output_full, preferred_element_type=single_float)
    ffn_out = lax.psum_scatter(
        unit_part.astype(jnp.bfloat16), "tensor", scatter_dimension=0, tiled=True
    ).astype(jnp.float32) + output_b.astype(single_float)
    resid_two = normed_one + ffn_out
    normed_two, norm_two_back = jax.vjp(
        layer_norm, resid_two, gain_two.astype(single_float), shift_two.astype(single_float)
    )
    layer_out = (normed_two * valid_own[:, None]).astype(bf16)
    query_reverse, key_back, value_back, out_back, inter_back, output_back = (
        lax.all_gather(query_w, "dp", axis=1, tiled=True),
        lax.all_gather(key_w, "dp", axis=0, tiled=True),
        lax.all_gather(value_w, "dp", axis=0, tiled=True),
        lax.all_gather(out_w, "dp", axis=1, tiled=True),
        lax.all_gather(inter_w, "dp", axis=0, tiled=True),
        lax.all_gather(output_w, "dp", axis=1, tiled=True),
    )
    grad_top = cotangent.astype(single_float) * valid_own[:, None]
    grad_resid_two, grad_gain_two, grad_shift_two = norm_two_back(grad_top)
    grad_ffn = grad_resid_two.astype(bf16)
    grad_output_b = jnp.sum(grad_ffn.astype(single_float), 0)
    full_grad_ffn = lax.all_gather(grad_ffn, "tensor", axis=0, tiled=True)
    grad_output_w = jnp.einsum(
        "tf,td->fd", active, full_grad_ffn, preferred_element_type=single_float
    )
    grad_active = jnp.einsum(
        "td,fd->tf", full_grad_ffn, output_back, preferred_element_type=single_float
    )
    grad_inner = gelu_back(grad_active)[0].astype(bf16)
    grad_inter_b_own = jnp.sum(grad_inner.astype(single_float), 0)
    grad_inter_w = jnp.einsum(
        "td,tf->df", full_normed, grad_inner, preferred_element_type=single_float
    )
    normed_part = jnp.einsum(
        "tf,df->td", grad_inner, inter_back, preferred_element_type=single_float
    )
    grad_normed = grad_resid_two + lax.psum_scatter(
        normed_part.astype(jnp.bfloat16), "tensor", scatter_dimension=0, tiled=True
    ).astype(jnp.float32)
    inter_grads, output_grads = (
        summed_on_arrival(grad_inter_w.astype(jnp.bfloat16), "dp", 0),
        summed_on_arrival(grad_output_w.astype(jnp.bfloat16), "dp", 1),
    )
    grad_resid_one, grad_gain_one, grad_shift_one = norm_one_back(grad_normed)
    grad_attended = grad_resid_one.astype(bf16)
    grad_out_b = jnp.sum(grad_attended.astype(single_float), 0)
    full_grad_att = lax.all_gather(grad_attended, "tensor", axis=0, tiled=True)
    grad_out_w = jnp.einsum(
        "tc,td->cd", mixed_flat, full_grad_att, preferred_element_type=single_float
    )
    grad_mixed = jnp.einsum(
        "td,cd->tc", full_grad_att, out_back, preferred_element_type=single_float
    ).astype(bf16)
    grad_mixed_heads = head_major(grad_mixed)

    def backward_step(carried, step_index):
        key_acc, value_acc = carried
        head_index, row_start, query_block, key_head, value_head, masked = block_parts(step_index)
        norm_row = lax.dynamic_index_in_dim(log_norm, step_index, 0, keepdims=False)
        attn_probs = jnp.exp(masked - norm_row[:, None])
        grad_head = lax.dynamic_index_in_dim(grad_mixed_heads, head_index, 0, keepdims=False)
        grad_block = lax.dynamic_slice_in_dim(grad_head, row_start, BLOCK, 0)
        grad_probs = jnp.einsum(
            "qc,kc->qk", grad_block, value_head, preferred_element_type=single_float
        )
        center = jnp.sum(attn_probs * grad_probs, -1, keepdims=True)
        grad_scores = (attn_probs * (grad_probs - center)).astype(bf16)
        grad_query = (
            jnp.dot(grad_scores, key_head, preferred_element_type=single_float) * score_scale
        )
        key_term = (
            jnp.einsum("qk,qc->kc", grad_scores, query_block, preferred_element_type=single_float)
            * score_scale
        )
        value_term = jnp.einsum(
            "qk,qc->kc", attn_probs.astype(bf16), grad_block, preferred_element_type=single_float
        )
        key_now = lax.dynamic_index_in_dim(key_acc, head_index, 0, keepdims=False)
        value_now = lax.dynamic_index_in_dim(value_acc, head_index, 0, keepdims=False)
        key_acc = lax.dynamic_update_index_in_dim(key_acc, key_now + key_term, head_index, 0)
        value_acc = lax.dynamic_update_index_in_dim(
            value_acc, value_now + value_term, head_index, 0
        )
        return ((key_acc, value_acc), grad_query.astype(bf16))

    start_carry = (
        jnp.zeros((heads_group, length, 2 * HD), single_float),
        jnp.zeros((heads_group, length, HD), single_float),
    )
    (key_acc, value_acc), grad_query_blocks = lax.scan(
        backward_step, start_carry, jnp.arange(heads_group * blocks)
    )
    grad_query_cat = grad_query_blocks.reshape(heads_group, length, 2 * HD)
    grad_to_word = token_major(grad_query_cat[:, :, :HD])
    grad_to_entity = token_major(grad_query_cat[:, :, HD:])
    key_grad_heads = (
        key_acc[:, :, :HD] * word_flag[None, :, None] + key_acc[:, :, HD:] * entity[None, :, None]
    )
    grad_keys = token_major(key_grad_heads).astype(bf16)
    grad_values = token_major(value_acc).astype(bf16)
    word_col = word_low[:, None]
    entity_col = entity_low[:, None]
    query_gradient_total = jnp.stack(
        [
            grad_to_word * word_col,
            grad_to_entity * word_col,
            grad_to_word * entity_col,
            grad_to_entity * entity_col,
        ],
        1,
    )
    query_weight_gradient = jnp.einsum(
        "kn,kqg->qng", complete_input, query_gradient_total, preferred_element_type=single_float
    )
    grad_query_b_own = jnp.sum(query_gradient_total.astype(single_float), 0)
    grad_key_w = jnp.einsum(
        "td,tc->dc", complete_input, grad_keys, preferred_element_type=single_float
    )
    grad_value_w = jnp.einsum(
        "td,tc->dc", complete_input, grad_values, preferred_element_type=single_float
    )
    grad_value_b_own = jnp.sum(grad_values.astype(single_float), 0)
    input_portion = jnp.einsum(
        "rgn,gmn->rm", query_gradient_total, query_reverse, preferred_element_type=single_float
    )
    input_portion = input_portion + jnp.einsum(
        "tc,dc->td", grad_keys, key_back, preferred_element_type=single_float
    )
    input_portion = input_portion + jnp.einsum(
        "tc,dc->td", grad_values, value_back, preferred_element_type=single_float
    )
    grad_hidden = grad_resid_one + lax.psum_scatter(
        input_portion.astype(jnp.bfloat16), "tensor", scatter_dimension=0, tiled=True
    ).astype(jnp.float32)
    query_grads, key_grads, value_grads, out_grads = (
        summed_on_arrival(query_weight_gradient.astype(jnp.bfloat16), "dp", 1),
        *side_by_side(
            (grad_key_w.astype(jnp.bfloat16), grad_value_w.astype(jnp.bfloat16)), "dp", 0, 1
        ),
        summed_on_arrival(grad_out_w.astype(jnp.bfloat16), "dp", 1),
    )
    query_b_full = lax.dynamic_update_slice_in_dim(
        jnp.zeros((4, width_full), single_float), grad_query_b_own, col_start, 1
    )
    value_b_full = lax.dynamic_update_slice_in_dim(
        jnp.zeros((width_full,), single_float), grad_value_b_own, col_start, 0
    )
    inter_b_full = lax.dynamic_update_slice_in_dim(
        jnp.zeros((ffn_group * groups,), single_float), grad_inter_b_own, unit_start, 0
    )
    (
        query_b_sum,
        value_b_sum,
        out_b_sum,
        gain_one_sum,
        shift_one_sum,
        inter_b_sum,
        output_b_sum,
        gain_two_sum,
        shift_two_sum,
    ) = lax.psum(
        (
            query_b_full,
            value_b_full,
            grad_out_b,
            grad_gain_one,
            grad_shift_one,
            inter_b_full,
            grad_output_b,
            grad_gain_two,
            grad_shift_two,
        ),
        ("dp", "tensor"),
    )
    return (
        layer_out,
        grad_hidden,
        query_grads,
        query_b_sum,
        key_grads,
        value_grads,
        value_b_sum,
        out_grads,
        out_b_sum,
        gain_one_sum,
        shift_one_sum,
        inter_grads,
        inter_b_sum,
        output_grads,
        output_b_sum,
        gain_two_sum,
        shift_two_sum,
    )


def solution(mesh):
    return jax.shard_map(
        local,
        mesh=mesh,
        in_specs=(
            P(("dp", "tensor"), None),
            P("dp"),
            P("dp"),
            P(("dp", "tensor"), None),
            P(None, "dp", "tensor"),
            P(),
            P("dp", "tensor"),
            P("dp", "tensor"),
            P(),
            P("tensor", "dp"),
            P(),
            P(),
            P(),
            P("dp", "tensor"),
            P(),
            P("tensor", "dp"),
            P(),
            P(),
            P(),
        ),
        out_specs=(
            P(("dp", "tensor"), None),
            P(("dp", "tensor"), None),
            P(None, "dp", "tensor"),
            P(),
            P("dp", "tensor"),
            P("dp", "tensor"),
            P(),
            P("tensor", "dp"),
            P(),
            P(),
            P(),
            P("dp", "tensor"),
            P(),
            P("tensor", "dp"),
            P(),
            P(),
            P(),
        ),
        check_vma=False,
    )
```

profile of v0, /device:TPU:0, one launch (start us, length us, event | category | flops | bytes accessed | tf_op | source)
XLA Modules:
  0.0 1315.4 jit_solution(16748227487391615398)
XLA Ops:
  10.7 11.3 all_gather.38
  22.0 10.4 all_gather.39
  32.5 10.6 all_gather.40
  50.6 53.7 %all-gather.8.cloned.1.call-done = bf16[2048,768]{1,0:T(8,128)(2,1)} async-done(((bf16[512,768]{1,0:T(8,128)(2,1)}), bf16[2048,768]{1,0:T(8,128)(2,1)}) %all-gather.8.cloned.1.call-update) | async-done | bytes 3145744 | tf_op jit(solution)/shard_map/all_gather | solution.py:100
  104.3 4.5 fusion.88
  134.2 161.5 %while.34 = (s32[]{:T(128)}, bf16[12,512,64]{1,2,0:T(8,128)(2,1)S(1)}, f32[12,512]{1,0:T(8,128)}, s32[12]{0:T(128)S(1)}, bf16[3,2048,128]{2,1,0:T(8,128)(2,1)}, ...) while((s32[]{:T(128)}, ...), condition=%wide.region_3.4_spmd.clone, body=%wide.region_0.3_spmd.clone.sunk | while | flops 415274528 | bytes 30635016 | solution.py:146
  300.6 3.9 convolution_convert_fusion.2
  305.1 58.4 %reduce-scatter.5.cloned.1.call-done = bf16[512,768]{1,0:T(8,128)(2,1)} async-done(((bf16[2048,768]{1,0:T(8,128)(2,1)}), bf16[512,768]{1,0:T(8,128)(2,1)}) %reduce-scatter.5.cloned.1.call-update) | async-done | bytes 786448 | tf_op jit(solution)/shard_map/reduce_scatter | solution.py:149
  369.4 20.0 %all-gather.14.cloned.1.call-done = bf16[768,768]{1,0:T(8,128)(2,1)} async-done(((bf16[96,768]{1,0:T(8,128)(2,1)}), bf16[768,768]{1,0:T(8,128)(2,1)}) %all-gather.14.cloned.1.call-update) | async-done | bytes 1179664 | tf_op jit(solution)/shard_map/all_gather | solution.py:90
  389.3 65.5 %all-gather.12.cloned.1.call-done = bf16[2048,768]{1,0:T(8,128)(2,1)} async-done(((bf16[512,768]{1,0:T(8,128)(2,1)}), bf16[2048,768]{1,0:T(8,128)(2,1)}) %all-gather.12.cloned.1.call-update) | async-done | bytes 3145744 | tf_op jit(solution)/shard_map/all_gather | solution.py:156
  454.9 19.0 %multiply_convert_fusion.1 = (bf16[2048,768]{1,0:T(8,128)(2,1)}, f32[2048,768]{1,0:T(8,128)}, f32[2048,768]{1,0:T(8,128)}) fusion(f32[768]{0:T(1024)S(1)} %dynamic-slice_convert_fusion, bf16[2048,768]{1,0:T(8,128)(2,1)} %all-gather.12.cloned.1.call-done, bf16[768,768]{1,0:T(8,128)(2,1)} %all-gather.14.cloned.1.call-done), kind=kOutput, calls=%fused_computation.73 | convolution fusion | flops 2519728128 | bytes 20057088 | tf_op jit(solution)/shard_map/dot_general | solution.py:157
  473.9 5.5 all-gather.16.cloned.1.call-done
  479.4 6.5 convolution_convert_fusion.1
  487.1 59.2 %reduce-scatter.7.cloned.1.call-done = bf16[512,768]{1,0:T(8,128)(2,1)} async-done(((bf16[2048,768]{1,0:T(8,128)(2,1)}), bf16[512,768]{1,0:T(8,128)(2,1)}) %reduce-scatter.7.cloned.1.call-update) | async-done | bytes 786448 | tf_op jit(solution)/shard_map/reduce_scatter | solution.py:161
  554.5 63.6 %all-gather.18.cloned.1.call-done = bf16[2048,768]{1,0:T(8,128)(2,1)} async-done(((bf16[512,768]{1,0:T(8,128)(2,1)}), bf16[2048,768]{1,0:T(8,128)(2,1)}) %all-gather.18.cloned.1.call-update) | async-done | bytes 3145744 | tf_op jit(solution)/shard_map/all_gather | solution.py:181
  618.2 11.1 convert_reduce_fusion
  631.0 4.0 convolution_convert_fusion
  635.1 59.0 %reduce-scatter.9.cloned.1.call-done = bf16[512,768]{1,0:T(8,128)(2,1)} async-done(((bf16[2048,768]{1,0:T(8,128)(2,1)}), bf16[512,768]{1,0:T(8,128)(2,1)}) %reduce-scatter.9.cloned.1.call-update) | async-done | bytes 786448 | tf_op jit(solution)/shard_map/reduce_scatter | solution.py:196
  702.4 63.5 %all-gather.20.cloned.1.call-done = bf16[2048,768]{1,0:T(8,128)(2,1)} async-done(((bf16[512,768]{1,0:T(8,128)(2,1)}), bf16[2048,768]{1,0:T(8,128)(2,1)}) %all-gather.20.cloned.1.call-update) | async-done | bytes 3145744 | tf_op jit(solution)/shard_map/all_gather | solution.py:206
  773.8 373.3 %while.35 = (s32[]{:T(128)}, f32[3,2048,128]{1,2,0:T(8,128)}, f32[3,2048,64]{1,2,0:T(8,128)}, bf16[12,512,128]{2,1,0:T(8,128)(2,1)}, s32[12]{0:T(128)S(1)}, /*in...) while((s32[]{:T(128)}, f32[3,2048,128]{1,2,0:T(8,128)}, ...), condition=%wide.region_17.18_spmd.clone, body=%wide.region_15.17_spmd.clone.sunk | while | flops 1083971072 | bytes 109198552 | solution.py:249
  777.1 3.8 fusion.154
  808.2 3.8 fusion.154
  839.4 3.8 fusion.154
  845.9 3.8 multiply_reduce_fusion.8
  870.5 3.8 fusion.154
  901.6 3.8 fusion.154
  932.7 3.8 fusion.154
  939.2 3.8 multiply_reduce_fusion.8
  963.8 3.8 fusion.154
  970.3 3.8 multiply_reduce_fusion.8
  994.9 3.8 fusion.154
  1026.0 3.8 fusion.154
  1057.1 3.8 fusion.154
  1088.2 3.8 fusion.154
  1094.7 3.8 multiply_reduce_fusion.8
  1119.3 3.8 fusion.154
  1147.1 4.2 fusion.85
  1163.5 4.3 fusion.51
  1169.7 5.6 convolution_convert_fusion.5
  1179.0 6.6 convolution_convert_fusion.6
  1185.6 10.2 all-to-all-done.4
  1196.8 4.3 all-to-all-start.3
  1201.4 3.8 convolution_convert_fusion.7
  1210.1 7.8 all-to-all-done.3
  1229.6 4.5 all-to-all-start.1
  1234.1 5.5 fusion.67
  1244.6 3.9 all-to-all-start
  1258.9 43.2 %all-reduce = (f32[4,768]{1,0:T(4,128)}, f32[768]{0:T(1024)}, f32[768]{0:T(1024)}, f32[768]{0:T(1024)}, f32[768]{0:T(1024)}, /*index=5*/f32[3072]{0:T(1024)}, f32[768]{0:T(1024)}, f32[768]{0:T(1024)}, f32[768]{0:T(1024)}) all-reduce(f32[4,768]{1,0:T(4,128)} %dynamic_update_slice.49, ...), channel_id=1, replica_groups=mesh['dp'=8,'tensor'=4] {'dp','tensor'}, use_global_device_ids=true, to_apply=%region_21.22 | all-reduce | flops 11520 | bytes 92160 | tf_op jit(solution)/shard_map/psum | solution.py:320
  (598 shorter events, 525.6 us)
Async XLA Ops:
  7.2 40.7 %all-gather.10.cloned.1.call-start = ((), (), s32[]{:S(2)}) async-start(), calls=%async_computation.10 | async-start | bytes 1769472 | tf_op jit(solution)/shard_map/all_gather | solution.py:86
  9.0 95.3 %all-gather.8.cloned.1.call-start = ((), (), s32[]{:S(2)}) async-start(), calls=%async_computation.9 | async-start | bytes 3932160 | tf_op jit(solution)/shard_map/all_gather | solution.py:100
  9.8 353.7 %reduce-scatter.5.cloned.1.call-start = ((), (), s32[]{:S(2)}) async-start(), calls=%async_computation.11 | async-start | bytes 3932160 | tf_op jit(solution)/shard_map/reduce_scatter | solution.py:149
  22.0 97.9 %copy-start.20 = (bf16[768,192]{1,0:T(8,128)(2,1)}, bf16[768,192]{1,0:T(8,128)(2,1)S(1)}, u32[]{:S(2)}) copy-start(bf16[768,192]{1,0:T(8,128)(2,1)S(1)} %all_gather.38) | copy-start | bytes 884740
  46.5 74.6 %copy-start.37 = (bf16[2048]{0:T(1024)(128)(2,1)}, bf16[2048]{0:T(1024)(128)(2,1)S(1)}, u32[]{:S(2)}) copy-start(bf16[2048]{0:T(1024)(128)(2,1)S(1)} %get-tuple-element.527) | copy-start | bytes 12292
  47.8 73.3 %copy-start.39 = (bf16[2048]{0:T(1024)(128)(2,1)}, bf16[2048]{0:T(1024)(128)(2,1)S(1)}, u32[]{:S(2)}) copy-start(bf16[2048]{0:T(1024)(128)(2,1)S(1)} %get-tuple-element.529) | copy-start | bytes 12292
  50.6 58.2 %copy-start.34 = (bf16[4,768,192]{1,2,0:T(8,128)(2,1)}, bf16[4,768,192]{1,2,0:T(8,128)(2,1)S(1)}, u32[]{:S(2)}) copy-start(bf16[4,768,192]{1,2,0:T(8,128)(2,1)S(1)} %copy.89) | copy-start | bytes 3538948
  112.3 7.6 copy-start.8
  300.5 63.0 %copy-start.5 = (bf16[512,768]{1,0:T(8,128)(2,1)S(1)}, bf16[512,768]{1,0:T(8,128)(2,1)}, u32[]{:S(2)}) copy-start(bf16[512,768]{1,0:T(8,128)(2,1)} %param.23) | copy-start | bytes 2359300
  304.4 84.9 %all-gather.14.cloned.1.call-start = ((), (), s32[]{:S(2)}) async-start(), calls=%async_computation.13 | async-start | bytes 1327104 | tf_op jit(solution)/shard_map/all_gather | solution.py:90
  305.0 149.9 %all-gather.12.cloned.1.call-start = ((), (), s32[]{:S(2)}) async-start(), calls=%async_computation.12 | async-start | bytes 3932160 | tf_op jit(solution)/shard_map/all_gather | solution.py:156
  368.0 111.4 %all-gather.16.cloned.1.call-start = ((), (), s32[]{:S(2)}) async-start(), calls=%async_computation.14 | async-start | bytes 1327104 | tf_op jit(solution)/shard_map/all_gather | solution.py:91
  368.6 177.7 %reduce-scatter.7.cloned.1.call-start = ((), (), s32[]{:S(2)}) async-start(), calls=%async_computation.15 | async-start | bytes 3932160 | tf_op jit(solution)/shard_map/reduce_scatter | solution.py:161
  485.9 132.3 %all-gather.18.cloned.1.call-start = ((), (), s32[]{:S(2)}) async-start(), calls=%async_computation.16 | async-start | bytes 3932160 | tf_op jit(solution)/shard_map/all_gather | solution.py:181
  551.6 142.4 %copy-start.41 = (f32[512]{0:T(512)}, f32[512]{0:T(512)S(1)}, u32[]{:S(2)}) copy-start(f32[512]{0:T(512)S(1)} %negate_multiply_fusion.2) | copy-start | bytes 6148
  554.5 139.6 %reduce-scatter.9.cloned.1.call-start = ((), (), s32[]{:S(2)}) async-start(), calls=%async_computation.17 | async-start | bytes 3932160 | tf_op jit(solution)/shard_map/reduce_scatter | solution.py:196
  618.2 12.8 copy-start.53
  635.0 130.8 %all-gather.20.cloned.1.call-start = ((), (), s32[]{:S(2)}) async-start(), calls=%async_computation.18 | async-start | bytes 3932160 | tf_op jit(solution)/shard_map/all_gather | solution.py:206
  697.5 68.4 %copy-start.22 = (bf16[192,768]{0,1:T(8,128)(2,1)S(1)}, bf16[192,768]{0,1:T(8,128)(2,1)}, u32[]{:S(2)}) copy-start(bf16[192,768]{0,1:T(8,128)(2,1)} %all_gather.40) | copy-start | bytes 884740
  702.1 603.8 %reduce-scatter.11.cloned.1.call-start = ((), (), s32[]{:S(2)}) async-start(), calls=%async_computation.19 | async-start | bytes 3932160 | tf_op jit(solution)/shard_map/reduce_scatter | solution.py:291
  773.8 13.5 %copy-start.6 = (bf16[3,2048,128]{2,1,0:T(8,128)(2,1)}, bf16[3,2048,128]{2,1,0:T(8,128)(2,1)S(1)}, u32[]{:S(2)}) copy-start(bf16[3,2048,128]{2,1,0:T(8,128)(2,1)S(1)} %get-tuple-element.757) | copy-start | bytes 4718596 | tf_op jit(solution)/shard_map/while
  804.9 13.5 %copy-start.6 = (bf16[3,2048,128]{2,1,0:T(8,128)(2,1)}, bf16[3,2048,128]{2,1,0:T(8,128)(2,1)S(1)}, u32[]{:S(2)}) copy-start(bf16[3,2048,128]{2,1,0:T(8,128)(2,1)S(1)} %get-tuple-element.757) | copy-start | bytes 4718596 | tf_op jit(solution)/shard_map/while
  828.5 5.2 copy-start.1
  836.1 13.5 %copy-start.6 = (bf16[3,2048,128]{2,1,0:T(8,128)(2,1)}, bf16[3,2048,128]{2,1,0:T(8,128)(2,1)S(1)}, u32[]{:S(2)}) copy-start(bf16[3,2048,128]{2,1,0:T(8,128)(2,1)S(1)} %get-tuple-element.757) | copy-start | bytes 4718596 | tf_op jit(solution)/shard_map/while
  867.2 13.5 %copy-start.6 = (bf16[3,2048,128]{2,1,0:T(8,128)(2,1)}, bf16[3,2048,128]{2,1,0:T(8,128)(2,1)S(1)}, u32[]{:S(2)}) copy-start(bf16[3,2048,128]{2,1,0:T(8,128)(2,1)S(1)} %get-tuple-element.757) | copy-start | bytes 4718596 | tf_op jit(solution)/shard_map/while
  890.8 5.3 copy-start.1
  898.3 13.5 %copy-start.6 = (bf16[3,2048,128]{2,1,0:T(8,128)(2,1)}, bf16[3,2048,128]{2,1,0:T(8,128)(2,1)S(1)}, u32[]{:S(2)}) copy-start(bf16[3,2048,128]{2,1,0:T(8,128)(2,1)S(1)} %get-tuple-element.757) | copy-start | bytes 4718596 | tf_op jit(solution)/shard_map/while
  921.9 5.2 copy-start.1
  929.4 13.5 %copy-start.6 = (bf16[3,2048,128]{2,1,0:T(8,128)(2,1)}, bf16[3,2048,128]{2,1,0:T(8,128)(2,1)S(1)}, u32[]{:S(2)}) copy-start(bf16[3,2048,128]{2,1,0:T(8,128)(2,1)S(1)} %get-tuple-element.757) | copy-start | bytes 4718596 | tf_op jit(solution)/shard_map/while
  953.0 5.3 copy-start.1
  960.5 13.5 %copy-start.6 = (bf16[3,2048,128]{2,1,0:T(8,128)(2,1)}, bf16[3,2048,128]{2,1,0:T(8,128)(2,1)S(1)}, u32[]{:S(2)}) copy-start(bf16[3,2048,128]{2,1,0:T(8,128)(2,1)S(1)} %get-tuple-element.757) | copy-start | bytes 4718596 | tf_op jit(solution)/shard_map/while
  984.1 5.2 copy-start.1
  991.6 13.5 %copy-start.6 = (bf16[3,2048,128]{2,1,0:T(8,128)(2,1)}, bf16[3,2048,128]{2,1,0:T(8,128)(2,1)S(1)}, u32[]{:S(2)}) copy-start(bf16[3,2048,128]{2,1,0:T(8,128)(2,1)S(1)} %get-tuple-element.757) | copy-start | bytes 4718596 | tf_op jit(solution)/shard_map/while
  1015.2 5.3 copy-start.1
  1022.7 13.5 %copy-start.6 = (bf16[3,2048,128]{2,1,0:T(8,128)(2,1)}, bf16[3,2048,128]{2,1,0:T(8,128)(2,1)S(1)}, u32[]{:S(2)}) copy-start(bf16[3,2048,128]{2,1,0:T(8,128)(2,1)S(1)} %get-tuple-element.757) | copy-start | bytes 4718596 | tf_op jit(solution)/shard_map/while
  1053.8 13.5 %copy-start.6 = (bf16[3,2048,128]{2,1,0:T(8,128)(2,1)}, bf16[3,2048,128]{2,1,0:T(8,128)(2,1)S(1)}, u32[]{:S(2)}) copy-start(bf16[3,2048,128]{2,1,0:T(8,128)(2,1)S(1)} %get-tuple-element.757) | copy-start | bytes 4718596 | tf_op jit(solution)/shard_map/while
  1084.9 13.5 %copy-start.6 = (bf16[3,2048,128]{2,1,0:T(8,128)(2,1)}, bf16[3,2048,128]{2,1,0:T(8,128)(2,1)S(1)}, u32[]{:S(2)}) copy-start(bf16[3,2048,128]{2,1,0:T(8,128)(2,1)S(1)} %get-tuple-element.757) | copy-start | bytes 4718596 | tf_op jit(solution)/shard_map/while
  1108.5 5.3 copy-start.1
  1116.0 13.5 %copy-start.6 = (bf16[3,2048,128]{2,1,0:T(8,128)(2,1)}, bf16[3,2048,128]{2,1,0:T(8,128)(2,1)S(1)}, u32[]{:S(2)}) copy-start(bf16[3,2048,128]{2,1,0:T(8,128)(2,1)S(1)} %get-tuple-element.757) | copy-start | bytes 4718596 | tf_op jit(solution)/shard_map/while
  1175.3 20.5 %all-to-all-start.4 = ((bf16[8,768,96]{1,2,0:T(8,128)(2,1)}), bf16[8,768,96]{1,2,0:T(8,128)(2,1)S(1)}, u32[]{:S(2)}, u32[]{:S(2)}) async-start(bf16[8,768,96]{1,2,0:T(8,128)(2,1)} %bitcast.42), calls=%async_computation.8 | async-start | bytes 2359296 | tf_op jit(solution)/shard_map/all_to_all | solution.py:17
  1179.0 22.1 %copy-start.45 = (f32[768]{0:T(1024)S(1)}, f32[768]{0:T(1024)}, u32[]{:S(2)}) copy-start(f32[768]{0:T(1024)} %get-tuple-element.491) | copy-start | bytes 9220
  1196.8 21.1 %all-to-all-start.3 = ((bf16[8,96,768]{2,1,0:T(8,128)(2,1)}), bf16[8,96,768]{2,1,0:T(8,128)(2,1)}, u32[]{:S(2)}, u32[]{:S(2)}) async-start(bf16[8,96,768]{2,1,0:T(8,128)(2,1)} %bitcast.40), calls=%async_computation.7 | async-start | bytes 2359296 | tf_op jit(solution)/shard_map/all_to_all | solution.py:17
  1201.1 6.4 copy-start.9
  1217.9 11.7 all-to-all-start.2
  1229.6 14.9 %all-to-all-start.1 = ((bf16[8,96,384]{2,1,0:T(8,128)(2,1)}), bf16[8,96,384]{2,1,0:T(8,128)(2,1)}, u32[]{:S(2)}, u32[]{:S(2)}) async-start(bf16[8,96,384]{2,1,0:T(8,128)(2,1)} %bitcast.229), calls=%async_computation.5 | async-start | bytes 1179648 | tf_op jit(solution)/shard_map/all_to_all | solution.py:17
  1244.2 7.4 copy-start.44
  1244.6 60.1 %all-to-all-start = ((bf16[8,4,96,192]{2,3,1,0:T(8,128)(2,1)}), bf16[8,4,96,192]{2,3,1,0:T(8,128)(2,1)S(1)}, u32[]{:S(2)}, u32[]{:S(2)}) async-start(bf16[8,4,96,192]{2,3,1,0:T(8,128)(2,1)} %bitcast.165), calls=%async_computation.4 | async-start | bytes 3145728 | tf_op jit(solution)/shard_map/all_to_all | solution.py:17
  1252.2 53.8 %copy-start.14 = (f32[512,768]{1,0:T(8,128)S(1)}, f32[512,768]{1,0:T(8,128)}, u32[]{:S(2)}) copy-start(f32[512,768]{1,0:T(8,128)} %copy-done.13) | copy-start | bytes 4718596
  (89 other events, 244.0 us)
Sparse Core Ops, SparseCore 0:
  10.5 28.7 all-gather.9
  40.8 63.4 all-gather.7
  304.6 58.8 reduce-scatter.4
  365.2 24.0 all-gather.13
  391.3 63.4 all-gather.11
  456.6 22.6 all-gather.15
  486.0 60.2 reduce-scatter.6
  554.6 63.5 all-gather.17
  635.1 58.8 reduce-scatter.8
  702.3 63.5 all-gather.19
  1168.0 58.8 reduce-scatter.10
where the time goes:
time: 1330 us; the launch traced here: 1320 us
  waiting for transfers between devices  472 us (35%)
  matrix products  336 us (25%)
  local copies, waits for them, and re-layouts  238 us (18%)
  loops' own time  80.1 us (6%)
  other arithmetic  77 us (6%)
  blocking collectives  75.4 us (6%)
  starting transfers between devices  20.8 us (2%)
  between operations  15.6 us (1%)
    dot_general x24, matrix products, block_parts(): jnp.einsum('qc,kc->qk', query_block, key_head, preferred_element_type=sin...  66 us
    all_gather x1, waiting for transfers between devices, local(): lax.all_gather(normed_one.astype(bf16), 'tensor', axis=0, tiled=True)  65.5 us
    all_gather x1, waiting for transfers between devices, local(): full_grad_ffn = lax.all_gather(grad_ffn, 'tensor', axis=0, tiled=True)  63.6 us
    all_gather x1, waiting for transfers between devices, local(): full_grad_att = lax.all_gather(grad_attended, 'tensor', axis=0, tiled=True)  63.5 us
    reduce_scatter x1, waiting for transfers between devices, local(): lax.psum_scatter(unit_part.astype(jnp.bfloat16), 'tensor', scatter_dimens...  59.2 us
    reduce_scatter x1, waiting for transfers between devices, local(): lax.psum_scatter(normed_part.astype(jnp.bfloat16), 'tensor', scatter_dime...  59 us
    reduce_scatter x1, waiting for transfers between devices, local(): lax.psum_scatter(attn_part.astype(jnp.bfloat16), 'tensor', scatter_dimens...  58.4 us
    all_gather x1, waiting for transfers between devices, local(): complete_input = lax.all_gather(hidden_in, 'tensor', axis=0, tiled=True)  53.7 us
  transfers between devices with their start and end apart: 16, of which 13 were waited for; matrix products, arithmetic and copies ran while one was open for 6% of the time, Pallas kernels for 0%

commit v1 on v0

v1 whole, which is shorter than its diff:
```python
import functools

import jax
import jax.numpy as jnp
from jax import lax
from jax.experimental import pallas as pl
from jax.experimental.pallas import tpu as pltpu
from jax.sharding import PartitionSpec as P

HD = 64
BLOCK = 512
LANES = 128
EPS = 1e-05
MASKED = -1e30
SQRT_HALF = 0.7071067811865476
INV_SQRT_2PI = 0.3989422804014327
VMEM_LIMIT = 60000 * 1024

f32 = jnp.float32
bf16 = jnp.bfloat16


def dot_nn(a, b):
    return lax.dot_general(a, b, (((1,), (0,)), ((), ())), preferred_element_type=f32)


def dot_nt(a, b):
    return lax.dot_general(a, b, (((1,), (1,)), ((), ())), preferred_element_type=f32)


def params(**kw):
    return pltpu.CompilerParams(vmem_limit_bytes=VMEM_LIMIT, **kw)


def cost(flops, nbytes, transcendentals=0):
    return pl.CostEstimate(flops=flops, bytes_accessed=nbytes, transcendentals=transcendentals)


def project_kernel(heads, x_ref, w_ref, b_ref, ent_ref, qc_ref, kc_ref, kv_ref):
    x = x_ref[...]
    ent = ent_ref[...] > 0.5
    lane = lax.broadcasted_iota(jnp.int32, (x.shape[0], LANES), 1)
    low_half = lane < HD
    keep = jnp.logical_xor(low_half, ent)
    for h in range(heads):
        base = 3 * LANES * h
        y = dot_nn(x, w_ref[:, base : base + 3 * LANES]) + b_ref[:, base : base + 3 * LANES]
        q = jnp.where(ent, y[:, LANES : 2 * LANES], y[:, :LANES])
        qc_ref[h] = q.astype(bf16) * (HD ** (-0.5))
        kv = y[:, 2 * LANES :].astype(bf16).astype(f32)
        kv_ref[h] = kv.astype(bf16)
        twice = jnp.where(low_half, kv, pltpu.roll(kv, HD, 1))
        kc_ref[h] = jnp.where(keep, twice, 0.0).astype(bf16)


def project(x, w, b, ent):
    tokens, width = x.shape
    columns = w.shape[1]
    heads = columns // (3 * LANES)
    out = jax.ShapeDtypeStruct((heads, tokens, LANES), bf16)
    spec = pl.BlockSpec((heads, BLOCK, LANES), lambda i: (0, i, 0))
    return pl.pallas_call(
        functools.partial(project_kernel, heads),
        grid=(tokens // BLOCK,),
        in_specs=[
            pl.BlockSpec((BLOCK, width), lambda i: (i, 0)),
            pl.BlockSpec((width, columns), lambda i: (0, 0)),
            pl.BlockSpec((1, columns), lambda i: (0, 0)),
            pl.BlockSpec((BLOCK, LANES), lambda i: (i, 0)),
        ],
        out_specs=[spec, spec, spec],
        out_shape=[out, out, out],
        compiler_params=params(),
        cost_estimate=cost(2 * tokens * width * columns, 2 * tokens * (width + columns)),
        name="project",
    )(x, w, b, ent)


def attend_kernel(me_ref, q_ref, kc_ref, kv_ref, bias_ref, out_ref, lse_ref, vt_ref):
    @pl.when(pl.program_id(1) == 0)
    def _():
        vt_ref[...] = kv_ref[0].T[HD:]

    scores = dot_nt(kc_ref[0], q_ref[0]) + bias_ref[:, :1]
    top = jnp.max(scores, 0, keepdims=True)
    exponent = jnp.exp(scores - top)
    total = jnp.sum(exponent, 0, keepdims=True)
    mixed = dot_nn(vt_ref[...], exponent.astype(bf16))
    out_ref[0] = (mixed / total).astype(bf16)
    lse_ref[0] = top + jnp.log(total)


def attend(me, qc, kc, kv, bias):
    heads, tokens, _ = qc.shape
    blocks = tokens // BLOCK
    full = pl.BlockSpec((1, tokens, LANES), lambda h, i, me: (h, 0, 0))
    return pl.pallas_call(
        attend_kernel,
        grid_spec=pltpu.PrefetchScalarGridSpec(
            num_scalar_prefetch=1,
            grid=(heads, blocks),
            in_specs=[
                pl.BlockSpec((1, BLOCK, LANES), lambda h, i, me: (h, i, 0)),
                full,
                full,
                pl.BlockSpec((tokens, LANES), lambda h, i, me: (0, 0)),
            ],
            out_specs=[
                pl.BlockSpec((1, HD, BLOCK), lambda h, i, me: (i ^ me[0], h, 0)),
                pl.BlockSpec((1, 1, BLOCK), lambda h, i, me: (h, 0, i)),
            ],
            scratch_shapes=[pltpu.VMEM((HD, tokens), bf16)],
        ),
        out_shape=[
            jax.ShapeDtypeStruct((blocks, heads * HD, BLOCK), bf16),
            jax.ShapeDtypeStruct((heads, 1, tokens), f32),
        ],
        compiler_params=params(),
        cost_estimate=cost(
            heads * tokens * tokens * 2 * 3 * LANES, heads * tokens * 8 * LANES, heads * tokens * tokens
        ),
        name="attend",
    )(me, qc, kc, kv, bias)


def attend_back_kernel(
    me_ref, q_ref, kc_ref, kv_ref, bias_ref, ent_ref, lse_ref, out_ref, go_ref,
    dq_ref, dkv_ref, kt_ref, dk_acc, dv_acc, go_pad,
):
    step = pl.program_id(1)

    @pl.when(step == 0)
    def _():
        kt_ref[...] = kc_ref[0].T
        go_pad[:HD] = jnp.zeros((HD, go_pad.shape[1]), bf16)
        dk_acc[...] = jnp.zeros_like(dk_acc)
        dv_acc[...] = jnp.zeros_like(dv_acc)

    go = go_ref[0]
    go_pad[HD:] = go
    delta = jnp.sum(go.astype(f32) * out_ref[0].astype(f32), 0, keepdims=True)
    q = q_ref[0]
    scores = dot_nt(kc_ref[0], q) + bias_ref[:, :1]
    probs = jnp.exp(scores - lse_ref[0])
    grad_probs = dot_nn(kv_ref[0], go_pad[...])
    grad_scores = (probs * (grad_probs - delta)).astype(bf16)
    dv_acc[...] += dot_nt(probs.astype(bf16), go_pad[...])
    dk_acc[...] += dot_nn(grad_scores, q)
    dq_ref[0] = (dot_nn(kt_ref[...], grad_scores) * (HD ** (-0.5))).T.astype(bf16)

    @pl.when(step == pl.num_programs(1) - 1)
    def _():
        lane = lax.broadcasted_iota(jnp.int32, dk_acc.shape, 1)
        dk = dk_acc[...]
        dk = jnp.where(ent_ref[...] > 0.5, pltpu.roll(dk, HD, 1), dk)
        dkv_ref[0] = jnp.where(lane < HD, dk, dv_acc[...]).astype(bf16)


def attend_back(me, qc, kc, kv, bias, ent, lse, mixed, grad_mixed):
    heads, tokens, _ = qc.shape
    blocks = tokens // BLOCK
    full = pl.BlockSpec((1, tokens, LANES), lambda h, i, me: (h, 0, 0))
    col = pl.BlockSpec((tokens, LANES), lambda h, i, me: (0, 0))
    rows = pl.BlockSpec((1, BLOCK, LANES), lambda h, i, me: (h, i, 0))
    slot = pl.BlockSpec((1, HD, BLOCK), lambda h, i, me: (i ^ me[0], h, 0))
    out = jax.ShapeDtypeStruct((heads, tokens, LANES), bf16)
    return pl.pallas_call(
        attend_back_kernel,
        grid_spec=pltpu.PrefetchScalarGridSpec(
            num_scalar_prefetch=1,
            grid=(heads, blocks),
            in_specs=[
                rows, full, full, col, col,
                pl.BlockSpec((1, 1, BLOCK), lambda h, i, me: (h, 0, i)),
                slot, slot,
            ],
            out_specs=[rows, full],
            scratch_shapes=[
                pltpu.VMEM((LANES, tokens), bf16),
                pltpu.VMEM((tokens, LANES), f32),
                pltpu.VMEM((tokens, LANES), f32),
                pltpu.VMEM((LANES, BLOCK), bf16),
            ],
        ),
        out_shape=[out, out],
        compiler_params=params(),
        cost_estimate=cost(
            heads * tokens * tokens * 2 * 5 * LANES, heads * tokens * 16 * LANES, heads * tokens * tokens
        ),
        name="attend_back",
    )(me, qc, kc, kv, bias, ent, lse, mixed, grad_mixed)


def normed(residual, gain, shift):
    center = residual - jnp.mean(residual, -1, keepdims=True)
    inv = lax.rsqrt(jnp.mean(center * center, -1, keepdims=True) + EPS)
    unit = center * inv
    return unit, inv, unit * gain + shift


def norm_back(grad, unit, inv, gain):
    scaled = grad * gain
    return (
        scaled
        - jnp.mean(scaled, -1, keepdims=True)
        - unit * jnp.mean(scaled * unit, -1, keepdims=True)
    ) * inv


def token_kernel(
    me_ref, m0, m1, m2, m3, hid_ref, cot_ref, valid_ref, w_ref, outb_ref, g1_ref, s1_ref, ib_ref,
    ob_ref, g2_ref, s2_ref,
    y_ref, mixt_ref, nb_ref, act_ref, gi_ref, gf_ref, ga_ref, gm_ref, gr_ref, sums_ref, gib_ref,
    slope_ref, outt_ref,
):
    me = me_ref[0]
    groups, width, _ = w_ref.shape
    ffn = act_ref.shape[2]
    gwidth = mixt_ref.shape[1]
    out_at = 2 * ffn
    for m, ref in enumerate((m0, m1, m2, m3)):
        mixt_ref[me ^ m] = ref[0]
    attended = outb_ref[...].astype(f32)
    for g in range(groups):
        part = dot_nt(mixt_ref[g].T, w_ref[g, :, out_at : out_at + gwidth])
        attended = attended + part.astype(bf16).astype(f32)
    gain_one = g1_ref[...].astype(f32)
    unit_one, inv_one, normed_one = normed(
        hid_ref[...].astype(f32) + attended, gain_one, s1_ref[...].astype(f32)
    )
    low_one = normed_one.astype(bf16)
    nb_ref[...] = low_one

    def forward(g, total):
        pre = dot_nn(low_one, w_ref[g, :, :ffn]) + ib_ref[g].astype(f32)
        cdf = 0.5 * (1.0 + lax.erf(pre * SQRT_HALF))
        slope_ref[g] = cdf + pre * (jnp.exp(-0.5 * pre * pre) * INV_SQRT_2PI)
        active = (pre * cdf).astype(bf16)
        act_ref[g] = active
        part = dot_nt(active, w_ref[g, :, ffn:out_at])
        return total + part.astype(bf16).astype(f32)

    ffn_out = lax.fori_loop(
        0, groups, forward, jnp.broadcast_to(ob_ref[...].astype(f32), normed_one.shape)
    )
    gain_two = g2_ref[...].astype(f32)
    valid = valid_ref[:, :1]
    unit_two, inv_two, normed_two = normed(normed_one + ffn_out, gain_two, s2_ref[...].astype(f32))
    y_ref[...] = (normed_two * valid).astype(bf16)
    grad_top = cot_ref[...].astype(f32) * valid
    grad_resid_two = norm_back(grad_top, unit_two, inv_two, gain_two)
    grad_ffn = grad_resid_two.astype(bf16)
    gf_ref[...] = grad_ffn

    def backward(g, total):
        grad_active = dot_nn(grad_ffn, w_ref[g, :, ffn:out_at])
        grad_inner = (slope_ref[g] * grad_active).astype(bf16)
        gi_ref[g] = grad_inner
        gib_ref[g] = jnp.sum(grad_inner.astype(f32), 0, keepdims=True)
        part = dot_nt(grad_inner, w_ref[g, :, :ffn])
        return total + part.astype(bf16).astype(f32)

    grad_normed = lax.fori_loop(0, groups, backward, grad_resid_two)
    grad_resid_one = norm_back(grad_normed, unit_one, inv_one, gain_one)
    gr_ref[...] = grad_resid_one
    grad_att = grad_resid_one.astype(bf16)
    ga_ref[...] = grad_att
    for g in range(groups):
        outt_ref[g] = w_ref[g, :, out_at : out_at + gwidth].T
    for m in range(groups):
        gm_ref[m] = dot_nt(outt_ref[me ^ m], grad_att).astype(bf16)
    rows = (
        grad_att.astype(f32),
        grad_normed * unit_one,
        grad_normed,
        grad_ffn.astype(f32),
        grad_top * unit_two,
        grad_top,
    )
    for at, value in enumerate(rows):
        sums_ref[at] = jnp.sum(value, 0, keepdims=True)


def per_token(me, mixed, hidden, cot, valid, w, out_b, gain1, shift1, inter_b, output_b, gain2, shift2):
    tokens, width = hidden.shape
    groups = w.shape[0]
    gwidth = mixed[0].shape[1]
    ffn = inter_b.shape[2]
    vmem = pl.BlockSpec(memory_space=pltpu.VMEM)
    shape = jax.ShapeDtypeStruct
    return pl.pallas_call(
        token_kernel,
        in_specs=[pl.BlockSpec(memory_space=pltpu.SMEM)] + [vmem] * 15,
        out_specs=[vmem] * 11,
        out_shape=[
            shape((tokens, width), bf16),
            shape((groups, gwidth, tokens), bf16),
            shape((tokens, width), bf16),
            shape((groups, tokens, ffn), bf16),
            shape((groups, tokens, ffn), bf16),
            shape((tokens, width), bf16),
            shape((tokens, width), bf16),
            shape((groups, gwidth, tokens), bf16),
            shape((tokens, width), f32),
            shape((6, 1, width), f32),
            shape((groups, 1, ffn), f32),
        ],
        scratch_shapes=[pltpu.VMEM((groups, tokens, ffn), f32), pltpu.VMEM((groups, gwidth, width), bf16)],
        compiler_params=params(),
        cost_estimate=cost(
            8 * tokens * width * ffn * groups + 4 * tokens * width * width,
            2 * w.size + 4 * tokens * ffn * groups,
            2 * tokens * ffn * groups,
        ),
        name="per_token",
    )(me, *mixed, hidden, cot, valid, w, out_b, gain1, shift1, inter_b, output_b, gain2, shift2)


def weight_grad_kernel(nb_ref, gf_ref, ga_ref, act_ref, gi_ref, mixt_ref, out_ref, nbt, gft, gat):
    ffn = act_ref.shape[2]
    gwidth = mixt_ref.shape[1]

    @pl.when(pl.program_id(0) == 0)
    def _():
        nbt[...] = nb_ref[...].T
        gft[...] = gf_ref[...].T
        gat[...] = ga_ref[...].T

    out_ref[0, :, :ffn] = dot_nn(nbt[...], gi_ref[0]).astype(bf16)
    out_ref[0, :, ffn : 2 * ffn] = dot_nn(gft[...], act_ref[0]).astype(bf16)
    out_ref[0, :, 2 * ffn : 2 * ffn + gwidth] = dot_nt(gat[...], mixt_ref[0]).astype(bf16)


def weight_grads(nb, gf, ga, act, gi, mixt):
    groups, tokens, ffn = act.shape
    width = nb.shape[1]
    gwidth = mixt.shape[1]
    whole = pl.BlockSpec((tokens, width), lambda g: (0, 0))
    group = pl.BlockSpec((1, tokens, ffn), lambda g: (g, 0, 0))
    columns = 2 * ffn + gwidth
    return pl.pallas_call(
        weight_grad_kernel,
        grid=(groups,),
        in_specs=[whole, whole, whole, group, group, pl.BlockSpec((1, gwidth, tokens), lambda g: (g, 0, 0))],
        out_specs=pl.BlockSpec((1, width, columns), lambda g: (g, 0, 0)),
        out_shape=jax.ShapeDtypeStruct((groups, width, columns), bf16),
        scratch_shapes=[pltpu.VMEM((width, tokens), bf16)] * 3,
        compiler_params=params(),
        cost_estimate=cost(2 * tokens * width * columns * groups, 2 * groups * width * columns),
        name="weight_grads",
    )(nb, gf, ga, act, gi, mixt)


def split_columns(heads, dq_ref, dkv_ref, ent):
    for h in range(heads):
        dq = dq_ref[h]
        nothing = jnp.zeros_like(dq)
        yield 3 * h, jnp.where(ent, nothing, dq)
        yield 3 * h + 1, jnp.where(ent, dq, nothing)
        yield 3 * h + 2, dkv_ref[h]


def input_grad_kernel(heads, me_ref, dq_ref, dkv_ref, ent_ref, w_ref, out_ref):
    ent = ent_ref[...] > 0.5
    cols = jnp.concatenate([c for _, c in split_columns(heads, dq_ref, dkv_ref, ent)], 1)
    out_ref[0] = dot_nt(cols, w_ref[...]).astype(bf16)


def input_grad(me, dq, dkv, ent, w):
    heads, tokens, _ = dq.shape
    width, columns = w.shape
    blocks = tokens // BLOCK
    stacked = pl.BlockSpec((heads, BLOCK, LANES), lambda i, me: (0, i, 0))
    return pl.pallas_call(
        functools.partial(input_grad_kernel, heads),
        grid_spec=pltpu.PrefetchScalarGridSpec(
            num_scalar_prefetch=1,
            grid=(blocks,),
            in_specs=[
                stacked,
                stacked,
                pl.BlockSpec((BLOCK, LANES), lambda i, me: (i, 0)),
                pl.BlockSpec((width, columns), lambda i, me: (0, 0)),
            ],
            out_specs=pl.BlockSpec((1, BLOCK, width), lambda i, me: (i ^ me[0], 0, 0)),
        ),
        out_shape=jax.ShapeDtypeStruct((blocks, BLOCK, width), bf16),
        compiler_params=params(),
        cost_estimate=cost(2 * tokens * width * columns, 2 * tokens * (columns + width)),
        name="input_grad",
    )(me, dq, dkv, ent, w)


def project_grad_kernel(heads, x_ref, dq_ref, dkv_ref, ent_ref, out_ref, bias_ref, acc_ref, bias_acc):
    step = pl.program_id(0)

    @pl.when(step == 0)
    def _():
        acc_ref[...] = jnp.zeros_like(acc_ref)
        bias_acc[...] = jnp.zeros_like(bias_acc)

    ent = ent_ref[...] > 0.5
    xt = x_ref[...].T
    for at, column in split_columns(heads, dq_ref, dkv_ref, ent):
        where = slice(LANES * at, LANES * (at + 1))
        acc_ref[:, where] += dot_nn(xt, column)
        bias_acc[:, where] += jnp.sum(column.astype(f32), 0, keepdims=True)

    @pl.when(step == pl.num_programs(0) - 1)
    def _():
        out_ref[...] = acc_ref[...].astype(bf16)
        bias_ref[...] = bias_acc[...]


def project_grad(x, dq, dkv, ent):
    heads, tokens, _ = dq.shape
    width = x.shape[1]
    columns = 3 * LANES * heads
    stacked = pl.BlockSpec((heads, BLOCK, LANES), lambda i: (0, i, 0))
    return pl.pallas_call(
        functools.partial(project_grad_kernel, heads),
        grid=(tokens // BLOCK,),
        in_specs=[
            pl.BlockSpec((BLOCK, width), lambda i: (i, 0)),
            stacked,
            stacked,
            pl.BlockSpec((BLOCK, LANES), lambda i: (i, 0)),
        ],
        out_specs=[
            pl.BlockSpec((width, columns), lambda i: (0, 0)),
            pl.BlockSpec((1, columns), lambda i: (0, 0)),
        ],
        out_shape=[
            jax.ShapeDtypeStruct((width, columns), bf16),
            jax.ShapeDtypeStruct((1, columns), f32),
        ],
        scratch_shapes=[pltpu.VMEM((width, columns), f32), pltpu.VMEM((1, columns), f32)],
        compiler_params=params(),
        cost_estimate=cost(2 * tokens * width * columns, 2 * tokens * (columns + width)),
        name="project_grad",
    )(x, dq, dkv, ent)


def local(
    hidden_in, token_types, lengths, cotangent, query_w, query_b, key_w, value_w, value_b, out_w,
    out_b, gain_one, shift_one, inter_w, inter_b, output_w, output_b, gain_two, shift_two,
):
    groups = lax.axis_size("tensor")
    dp = lax.axis_size("dp")
    z = lax.axis_index("tensor")
    d = lax.axis_index("dp")
    half = groups // 2
    core = d % 2
    upper = z // half
    me = z % half + half * core
    me_ref = me.astype(jnp.int32).reshape(1)
    own_rows, width = hidden_in.shape
    length = own_rows * groups
    gwidth = query_w.shape[2]
    heads = gwidth // HD
    ffn = inter_w.shape[1]
    total = dp * groups

    def at(dev):
        return dev // groups, dev % groups

    def device(dd, zz):
        return dd * groups + zz

    def swapped(dev):
        dd, zz = at(dev)
        return device(dd - dd % 2 + zz // half, zz % half + half * (dd % 2))

    def member(dev, mask):
        dd, zz = at(dev)
        j = (zz % half + half * (dd % 2)) ^ mask
        return device(dd - dd % 2 + j // half, zz - zz % half + j % half)

    relocation = [(i, swapped(i)) for i in range(total)]

    def relocate(value):
        return lax.ppermute(value, ("dp", "tensor"), relocation)

    def to_member(value, mask):
        return lax.ppermute(value, ("dp", "tensor"), [(i, member(i, mask)) for i in range(total)])

    facts = jnp.concatenate([token_types, lengths])
    other = lax.ppermute(facts, "dp", [(i, i ^ 1) for i in range(dp)])
    facts = jnp.where(core == upper, facts, other)
    entity = facts[:length].astype(f32)
    positions = jnp.arange(length, dtype=jnp.int32)
    valid = positions < facts[length]
    ent = jnp.broadcast_to(entity[:, None], (length, LANES))
    bias = jnp.broadcast_to(jnp.where(valid, 0.0, MASKED)[:, None], (length, LANES)).astype(f32)
    valid_own = lax.dynamic_slice_in_dim(valid.astype(f32), me * own_rows, own_rows)
    valid_own = jnp.broadcast_to(valid_own[:, None], (own_rows, LANES))

    rows = key_w.shape[0]
    own_project = jnp.concatenate(
        [
            query_w.reshape(4, rows, heads, HD).transpose(1, 2, 0, 3),
            key_w.reshape(rows, heads, 1, HD),
            value_w.reshape(rows, heads, 1, HD),
        ],
        2,
    ).reshape(rows, 6 * gwidth)
    own_ffn = jnp.concatenate([inter_w, output_w.T, out_w.T], 1)

    hidden = relocate(hidden_in)
    from_core = to_member(hidden, half)
    pair = jnp.stack([hidden, from_core])
    other_pair = to_member(pair, 1)
    pieces = [pair[0], other_pair[0], pair[1], other_pair[1]]
    x = jnp.zeros((groups, own_rows, width), bf16)
    for m, piece in enumerate(pieces):
        x = lax.dynamic_update_index_in_dim(x, piece, me ^ m, 0)
    x = x.reshape(length, width)

    w_project = relocate(lax.all_gather(own_project, "dp", axis=0, tiled=True))
    w_ffn = lax.all_gather(lax.all_gather(own_ffn, "tensor"), "dp", axis=1, tiled=True)

    query_b_own = lax.dynamic_slice_in_dim(query_b, me * gwidth, gwidth, 1)
    value_b_own = lax.dynamic_slice_in_dim(value_b, me * gwidth, gwidth)
    b_project = jnp.concatenate(
        [
            query_b_own.reshape(4, heads, HD).transpose(1, 0, 2),
            jnp.zeros((heads, 1, HD), bf16),
            value_b_own.reshape(heads, 1, HD),
        ],
        1,
    ).reshape(1, 6 * gwidth).astype(f32)

    qc, kc, kv = project(x, w_project, b_project, ent)
    mixed, lse = attend(me_ref, qc, kc, kv, bias)
    mixed_own = [mixed[:1]] + [to_member(mixed[m : m + 1], m) for m in range(1, groups)]
    cot = relocate(cotangent)
    row = lambda v: v.reshape(1, -1)
    y, mixt, nb, act, gi, gf, ga, gm, grad_resid_one, sums, gib = per_token(
        me_ref, mixed_own, hidden, cot, valid_own, w_ffn, row(out_b), row(gain_one), row(shift_one),
        inter_b.reshape(groups, 1, ffn), row(output_b), row(gain_two), row(shift_two),
    )
    layer_out = relocate(y)
    grad_mixed = jnp.concatenate([gm[:1]] + [to_member(gm[m : m + 1], m) for m in range(1, groups)])
    ffn_grads = weight_grads(nb, gf, ga, act, gi, mixt)
    ffn_grads = lax.psum_scatter(ffn_grads, "tensor", scatter_dimension=0, tiled=False)
    ffn_grads = lax.psum_scatter(ffn_grads, "dp", scatter_dimension=0, tiled=True).astype(f32)

    dq, dkv = attend_back(me_ref, qc, kc, kv, bias, ent, lse, mixed, grad_mixed)
    partial = input_grad(me_ref, dq, dkv, ent, w_project)
    project_grads, project_sums = project_grad(x, dq, dkv, ent)

    arrived = to_member(partial[half:], half)
    near = partial[:half].astype(f32) + arrived.astype(f32)
    arrived = to_member(near[1].astype(bf16), 1)
    grad_hidden = grad_resid_one + near[0] + arrived.astype(f32)
    grad_hidden = relocate(grad_hidden.astype(bf16)).astype(f32)

    project_grads = relocate(project_grads)
    project_grads = lax.psum_scatter(project_grads, "dp", scatter_dimension=0, tiled=True).astype(f32)
    project_grads = project_grads.reshape(rows, heads, 6, HD)
    query_grads = project_grads[:, :, :4].transpose(2, 0, 1, 3).reshape(4, rows, gwidth)
    key_grads = project_grads[:, :, 4].reshape(rows, gwidth)
    value_grads = project_grads[:, :, 5].reshape(rows, gwidth)

    inter_grads = ffn_grads[:, :ffn]
    output_grads = ffn_grads[:, ffn : 2 * ffn].T
    out_grads = ffn_grads[:, 2 * ffn :].T

    project_sums = project_sums.reshape(heads, 6, HD)
    sum_rows = jnp.concatenate(
        [
            project_sums[:, :4].transpose(1, 0, 2).reshape(4, gwidth),
            project_sums[:, 5].reshape(1, gwidth),
        ]
    )
    sum_rows = lax.dynamic_update_slice_in_dim(jnp.zeros((5, width), f32), sum_rows, me * gwidth, 1)
    flat = jnp.concatenate([sum_rows, sums.reshape(6, width), gib.reshape(groups, ffn)])
    flat = lax.psum(flat, ("dp", "tensor"))
    return (
        layer_out,
        grad_hidden,
        query_grads,
        flat[:4],
        key_grads,
        value_grads,
        flat[4],
        out_grads,
        flat[5],
        flat[6],
        flat[7],
        inter_grads,
        flat[11:].reshape(groups * ffn),
        output_grads,
        flat[8],
        flat[9],
        flat[10],
    )


def solution(mesh):
    weights = P("dp", "tensor")
    tokens = P(("dp", "tensor"), None)
    return jax.shard_map(
        local,
        mesh=mesh,
        in_specs=(
            tokens, P("dp"), P("dp"), tokens, P(None, "dp", "tensor"), P(), weights, weights, P(),
            P("tensor", "dp"), P(), P(), P(), weights, P(), P("tensor", "dp"), P(), P(), P(),
        ),
        out_specs=(
            tokens, tokens, P(None, "dp", "tensor"), P(), weights, weights, P(), P("tensor", "dp"),
            P(), P(), P(), weights, P(), P("tensor", "dp"), P(), P(), P(),
        ),
        check_vma=False,
    )
```

time: 1330 us -> 556 us (0.42)
  matrix products: 336 us -> 0 us
  waiting for transfers between devices: 472 us -> 143 us
  local copies, waits for them, and re-layouts: 238 us -> 35 us
  starting transfers between devices: 20.8 us -> 174 us
  Pallas kernels: 0 us -> 132 us
  loops' own time: 80.1 us -> 0 us
  other arithmetic: 77 us -> 10.1 us
  blocking collectives: 75.4 us -> 44.3 us
    dot_general x101 -> x0, matrix products: 332 us -> none  [the longest x24 66 us: block_parts(): jnp.einsum('qc,kc->qk', query_block, key_head, preferred_element_type=sin...]
    all_gather x7 -> x3, waiting for transfers between devices: 272 us -> 32.7 us  [the longest x1 32.7 us: local(): lax.all_gather(own_ffn, 'tensor')]
    ppermute x0 -> x17, starting transfers between devices: none -> 174 us  [the longest x10 158 us: to_member(): lax.ppermute(value, ('dp', 'tensor'), [(i, member(i, mask)) for i in rang...]
    reduce_scatter x4 -> x3, waiting for transfers between devices: 177 us -> 7.03 us  [the longest x1 7.03 us: local(): lax.psum_scatter(ffn_grads, 'dp', scatter_dimension=0, tiled=True)]
    pallas_call x0 -> x7, Pallas kernels: none -> 132 us  [the longest x1 38.6 us: attend_back(): pl.pallas_call(attend_back_kernel, grid_spec=pltpu.PrefetchScalarGridSpec...]
    ppermute x0 -> x17, waiting for transfers between devices: none -> 104 us  [the longest x10 104 us: to_member(): lax.ppermute(value, ('dp', 'tensor'), [(i, member(i, mask)) for i in rang...]
    dynamic_slice x72 -> x2, local copies, waits for them, and re-layouts: 83.8 us -> 0.83 us  [the longest x1 0.76 us: local(): value_b_own = lax.dynamic_slice_in_dim(value_b, me * gwidth, gwidth)]
    another operation x2 -> x0, loops' own time: 80.1 us -> none  [the longest x1 48.2 us: local(): lax.scan(backward_step, start_carry, jnp.arange(heads_group * blocks))]
  transfers between devices with their start and end apart: 16 -> 23, of which waited for: 13 -> 10; matrix products, arithmetic and copies ran while one was open for 6% -> 6% of each run, Pallas kernels for 0% -> 17%
where the time goes in v1:
time: 556 us; the launch traced here: 554 us
  starting transfers between devices  174 us (31%)
  waiting for transfers between devices  143 us (26%)
  Pallas kernels  132 us (24%)
  blocking collectives  44.3 us (8%)
  local copies, waits for them, and re-layouts  35 us (6%)
  between operations  15.3 us (3%)
  other arithmetic  10.1 us (2%)
    ppermute x10, starting transfers between devices, to_member(): lax.ppermute(value, ('dp', 'tensor'), [(i, member(i, mask)) for i in rang...  158 us
    ppermute x10, waiting for transfers between devices, to_member(): lax.ppermute(value, ('dp', 'tensor'), [(i, member(i, mask)) for i in rang...  104 us
    psum x1, blocking collectives, local(): flat = lax.psum(flat, ('dp', 'tensor'))  44.3 us
    pallas_call x1, Pallas kernels, attend_back(): pl.pallas_call(attend_back_kernel, grid_spec=pltpu.PrefetchScalarGridSpec...  38.6 us
    all_gather x1, waiting for transfers between devices, local(): lax.all_gather(own_ffn, 'tensor')  32.7 us
    pallas_call x1, Pallas kernels, per_token(): pl.pallas_call(token_kernel, in_specs=[pl.BlockSpec(memory_space=pltpu.SM...  28.2 us
    pallas_call x1, Pallas kernels, attend(): pl.pallas_call(attend_kernel, grid_spec=pltpu.PrefetchScalarGridSpec(num_...  24.6 us
    ppermute x6, starting transfers between devices, relocate(): return lax.ppermute(value, ('dp', 'tensor'), relocation)  15.1 us
  transfers between devices with their start and end apart: 23, of which 10 were waited for; matrix products, arithmetic and copies ran while one was open for 6% of the time, Pallas kernels for 17%

profile of v1, /device:TPU:0, one launch (start us, length us, event | category | flops | bytes accessed | tf_op | source)
XLA Modules:
  0.0 554.5 jit_solution(15160313958020983345)
XLA Ops:
  7.3 0.9 copy.65
  8.1 1.7 pad_maximum_fusion.2
  10.0 1.1 copy.58
  11.1 1.0 copy.59
  12.0 0.9 copy.60
  14.0 32.7 %all-gather.9.cloned.1.call-done = bf16[384,1728]{1,0:T(8,128)(2,1)} async-done(((bf16[96,1728]{1,0:T(8,128)(2,1)}), bf16[384,1728]{1,0:T(8,128)(2,1)}) %all-gather.9.cloned.1.call-update) | async-done | bytes 1327120 | tf_op jit(solution)/shard_map/all_gather | solution.py:520
  47.7 21.0 %collective-permute-start.1 = (bf16[512,768]{1,0:T(8,128)(2,1)S(1)}, bf16[512,768]{1,0:T(8,128)(2,1)S(1)}, u32[]{:S(2)}, u32[]{:S(2)}) collective-permute-start(bf16[512,768]{1,0:T(8,128)(2,1)S(1)} %collective-permute-done.hid_ref), channel_id=1, source_target_pairs={{0,4},{1,5},{2,6},{3,7},{4,0},{5,1},{6,2},{7,3},{8,12},{9,13},{10,... | collective-permute-start | bytes 2359304 | tf_op jit(solution)/shard_map/ppermute | solution.py:485
  68.7 1.9 collective-permute-done.1
  70.6 1.4 pad_maximum_fusion
  73.1 7.4 %collective-permute-start.8 = (bf16[512,768]{1,0:T(8,128)(2,1)}, bf16[512,768]{1,0:T(8,128)(2,1)}, u32[]{:S(2)}, u32[]{:S(2)}) collective-permute-start(bf16[512,768]{1,0:T(8,128)(2,1)} %param.22), channel_id=1, source_target_pairs={{0,0},{1,1},{2,4},{3,5},{4,2},{5,3},{6,6},{7,7},{8,8},{9,9},{10,12... | collective-permute-start | bytes 2359304 | tf_op jit(solution)/shard_map/ppermute | solution.py:482
  81.7 2.3 collective-permute-start.3
  90.4 46.0 %collective-permute-done.2 = bf16[2,512,768]{2,1,0:T(8,128)(2,1)} collective-permute-done((bf16[2,512,768]{2,1,0:T(8,128)(2,1)}, bf16[2,512,768]{2,1,0:T(8,128)(2,1)}, u32[]{:S(2)}, u32[]{:S(2)}) %collective-permute-start.2) | collective-permute-done | bytes 1572896 | tf_op jit(solution)/shard_map/ppermute | solution.py:485
  136.4 1.2 slice_dynamic-update-slice_fusion.1
  137.6 1.2 slice_dynamic-update-slice_fusion
  138.9 1.8 broadcast_in_dim.45.ent_ref
  141.5 8.9 %project.1 = (bf16[3,2048,128]{2,1,0:T(8,128)(2,1)}, bf16[3,2048,128]{2,1,0:T(8,128)(2,1)}, bf16[3,2048,128]{2,1,0:T(8,128)(2,1)}) custom-call(bf16[2048,768]{1,0:T(8,128)(2,1)} %bitcast.50, bf16[768,1152]{1,0:T(8,128)(2,1)} %copy-done.23, f32[1,1152]{1,0:T(1,128)} %reshape.149.b_ref, f32[2048,128]{1,0:T(8,128)} %broadcast_in_dim.45.ent_ref), custom_call_target="tpu_custom_call" | custom-call | flops 3623878656 | bytes 7864320 | tf_op jit(solution)/shard_map/project/pallas_call | solution.py:62
  150.4 1.3 broadcast_in_dim.48.bias_ref
  151.7 24.6 %attend.1 = (bf16[4,192,512]{2,1,0:T(8,128)(2,1)}, f32[3,1,2048]{2,1,0:T(1,128)}) custom-call(s32[1]{0:T(128)} %bitcast.me_ref, bf16[3,2048,128]{2,1,0:T(8,128)(2,1)} %get-tuple-element.37.q_ref, bf16[3,2048,128]{2,1,0:T(8,128)(2,1)} %get-tuple-element.38.kc_ref, bf16[3,2048,128]{2,1,0:T(8,128)(2,1)} %get-tuple-element.39.kv_ref, ...), custom_call_target="tpu_custom_call" | custom-call | flops 9663676416 | bytes 6291456 | tf_op jit(solution)/shard_map/attend/pallas_call | solution.py:97
  176.2 1.9 fusion.5
  178.2 2.1 collective-permute-start.7
  181.1 4.9 collective-permute-done.5.m1
  186.0 1.3 collective-permute-done.7.m3
  188.1 28.2 %per_token.1 = (bf16[512,768]{1,0:T(8,128)(2,1)}, bf16[4,192,512]{2,1,0:T(8,128)(2,1)}, bf16[512,768]{1,0:T(8,128)(2,1)}, bf16[4,512,768]{2,1,0:T(8,128)(2,1)}, ...) custom-call(s32[1]{0:T(128)} %bitcast.me_ref, ...), custom_call_target="tpu_custom_call" | custom-call | flops 10871635968 | bytes 16908288 | tf_op jit(solution)/shard_map/per_token/pallas_call | solution.py:291
  216.4 12.0 %weight_grads.1 = bf16[4,768,1728]{2,1,0:T(8,128)(2,1)} custom-call(bf16[512,768]{1,0:T(8,128)(2,1)} %get-tuple-element.51.nb_ref, bf16[512,768]{1,0:T(8,128)(2,1)} %get-tuple-element.52.gf_ref, bf16[512,768]{1,0:T(8,128)(2,1)} %get-tuple-element.53.ga_ref, bf16[4,512,768]{2,1,0:T(8,128)(2,1)} %get-tuple-element.54.act_ref, ...), custom_call_target="tpu_custom_call" | custom-call | flops 5435817984 | bytes 10616832 | tf_op jit(solution)/shard_map/weight_grads/pallas_call | solution.py:341
  228.5 1.1 copy-done.11
  229.6 1.1 collective-permute-start.10
  231.0 1.3 collective-permute-start.12
  232.3 4.8 collective-permute-done.10
  237.1 16.6 %collective-permute-done.12 = bf16[1,192,512]{2,1,0:T(8,128)(2,1)S(1)} collective-permute-done((bf16[1,192,512]{2,1,0:T(8,128)(2,1)S(1)}, bf16[1,192,512]{2,1,0:T(8,128)(2,1)S(1)}, u32[]{:S(2)}, u32[]{:S(2)}) %collective-permute-start.12) | collective-permute-done | bytes 196640 | tf_op jit(solution)/shard_map/ppermute | solution.py:485
  253.7 1.0 pad_maximum_fusion.1.go_ref
  254.7 38.6 %attend_back.1 = (bf16[3,2048,128]{2,1,0:T(8,128)(2,1)}, bf16[3,2048,128]{2,1,0:T(8,128)(2,1)}) custom-call(s32[1]{0:T(128)} %bitcast.me_ref, bf16[3,2048,128]{2,1,0:T(8,128)(2,1)} %get-tuple-element.37.q_ref, bf16[3,2048,128]{2,1,0:T(8,128)(2,1)} %get-tuple-element.38.kc_ref, bf16[3,2048,128]{2,1,0:T(8,128)(2,1)} %get-tuple-element.39.kv_ref, ...), custom_call_target="tpu_custom_call" | custom-call | flops 16106127360 | bytes 12582912 | tf_op jit(solution)/shard_map/attend_back/pallas_call | solution.py:167
  293.3 11.5 %project_grad.1 = (bf16[768,1152]{1,0:T(8,128)(2,1)}, f32[1,1152]{1,0:T(1,128)}) custom-call(bf16[2048,768]{1,0:T(8,128)(2,1)} %bitcast.51, bf16[3,2048,128]{2,1,0:T(8,128)(2,1)} %get-tuple-element.45.dq_ref, bf16[3,2048,128]{2,1,0:T(8,128)(2,1)} %get-tuple-element.46.dkv_ref, f32[2048,128]{1,0:T(8,128)} %broadcast_in_dim.45.ent_ref), custom_call_target="tpu_custom_call" | custom-call | flops 3623878656 | bytes 7864320 | tf_op jit(solution)/shard_map/project_grad/pallas_call | solution.py:420
  304.8 2.1 collective-permute-start.16
  306.9 1.2 copy-done.8
  308.2 8.4 %input_grad.1 = bf16[4,512,768]{2,1,0:T(8,128)(2,1)} custom-call(s32[1]{0:T(128)} %bitcast.me_ref, bf16[3,2048,128]{2,1,0:T(8,128)(2,1)} %get-tuple-element.45.dq_ref, bf16[3,2048,128]{2,1,0:T(8,128)(2,1)} %get-tuple-element.46.dkv_ref, f32[2048,128]{1,0:T(8,128)} %broadcast_in_dim.45.ent_ref, bf16[768,1152]{1,0:T(8,128)(2,1)} %copy-done.23), custom_call_target="tpu_custom_call" | custom-call | flops 3623878656 | bytes 7864320 | tf_op jit(solution)/shard_map/input_grad/pallas_call | solution.py:374
  316.6 2.8 slice.138
  319.4 130.7 %collective-permute-start.13 = (bf16[2,512,768]{2,1,0:T(8,128)(2,1)}, bf16[2,512,768]{2,1,0:T(8,128)(2,1)}, u32[]{:S(2)}, u32[]{:S(2)}) collective-permute-start(bf16[2,512,768]{2,1,0:T(8,128)(2,1)} %slice.138), channel_id=1, source_target_pairs={{0,4},{1,5},{2,6},{3,7},{4,0},{5,1},{6,2},{7,3},{8,12},{9,13},{10,... | collective-permute-start | bytes 4718600 | tf_op jit(solution)/shard_map/ppermute | solution.py:485
  450.1 3.4 collective-permute-done.13
  453.4 1.8 convert_add_fusion
  455.4 1.9 collective-permute-start.14
  457.2 1.8 collective-permute-start.9
  459.0 24.7 %collective-permute-done.14 = bf16[512,768]{1,0:T(8,128)(2,1)S(1)} collective-permute-done((bf16[512,768]{1,0:T(8,128)(2,1)S(1)}, bf16[512,768]{1,0:T(8,128)(2,1)S(1)}, u32[]{:S(2)}, u32[]{:S(2)}) %collective-permute-start.14) | collective-permute-done | bytes 786464 | tf_op jit(solution)/shard_map/ppermute | solution.py:485
  485.4 44.3 %psum.7 = f32[15,768]{1,0:T(8,128)S(1)} all-reduce(f32[15,768]{1,0:T(8,128)S(1)} %pad_maximum_fusion.4), channel_id=1, replica_groups=mesh['dp'=8,'tensor'=4] {'dp','tensor'}, use_global_device_ids=true, to_apply=%region_1.2 | all-reduce | flops 11520 | bytes 92160 | tf_op jit(solution)/shard_map/psum | solution.py:578
  531.6 1.3 convert_element_type.43
  532.8 1.1 copy.67
  534.0 0.9 copy.70
  536.4 7.0 %reduce-scatter.8.cloned.1.call-done = bf16[96,1728]{1,0:T(8,128)(2,1)} async-done(((bf16[768,1728]{1,0:T(8,128)(2,1)}), bf16[96,1728]{1,0:T(8,128)(2,1)}) %reduce-scatter.8.cloned.1.call-update) | async-done | bytes 331792 | tf_op jit(solution)/shard_map/reduce_scatter | solution.py:546
  543.5 1.1 convert_element_type.44
  (145 shorter events, 21.0 us)
Async XLA Ops:
  7.2 73.4 %copy-start = (bf16[4,768]{1,0:T(4,128)(2,1)S(1)}, bf16[4,768]{1,0:T(4,128)(2,1)}, u32[]{:S(2)}) copy-start(bf16[4,768]{1,0:T(4,128)(2,1)} %param.24) | copy-start | bytes 18436
  7.2 39.5 %all-gather.9.cloned.1.call-start = ((), (), s32[]{:S(2)}) async-start(), calls=%async_computation.8 | async-start | bytes 1720320 | tf_op jit(solution)/shard_map/all_gather | solution.py:520
  9.9 71.7 %all-gather.5.cloned.1.call-start = ((), (), s32[]{:S(2)}) async-start(), calls=%async_computation.3 | async-start | bytes 1990656 | tf_op jit(solution)/shard_map/all_gather | solution.py:519
  11.1 35.8 %copy-start.24 = (bf16[512,768]{1,0:T(8,128)(2,1)S(1)}, bf16[512,768]{1,0:T(8,128)(2,1)}, u32[]{:S(2)}) copy-start(bf16[512,768]{1,0:T(8,128)(2,1)} %param.19) | copy-start | bytes 2359300
  14.0 173.3 %all-gather.7.cloned.1.call-start = ((), (), s32[]{:S(2)}) async-start(), calls=%async_computation.4 | async-start | bytes 12386304 | tf_op jit(solution)/shard_map/all_gather | solution.py:520
  46.8 25.9 %copy-start.14 = (s32[2048]{0:T(1024)S(1)}, s32[2048]{0:T(1024)}, u32[]{:S(2)}) copy-start(s32[2048]{0:T(1024)} %param.20) | copy-start | bytes 24580
  46.8 38.0 %copy-start.15 = (bf16[3072]{0:T(1024)(128)(2,1)S(1)}, bf16[3072]{0:T(1024)(128)(2,1)}, u32[]{:S(2)}) copy-start(bf16[3072]{0:T(1024)(128)(2,1)} %param.33) | copy-start | bytes 18436
  46.8 38.6 %copy-start.17 = (bf16[768]{0:T(1024)(128)(2,1)S(1)}, bf16[768]{0:T(1024)(128)(2,1)}, u32[]{:S(2)}) copy-start(bf16[768]{0:T(1024)(128)(2,1)} %param.29) | copy-start | bytes 4612
  46.8 39.1 %copy-start.18 = (bf16[768]{0:T(1024)(128)(2,1)S(1)}, bf16[768]{0:T(1024)(128)(2,1)}, u32[]{:S(2)}) copy-start(bf16[768]{0:T(1024)(128)(2,1)} %param.30) | copy-start | bytes 4612
  46.8 39.7 %copy-start.19 = (bf16[768]{0:T(1024)(128)(2,1)S(1)}, bf16[768]{0:T(1024)(128)(2,1)}, u32[]{:S(2)}) copy-start(bf16[768]{0:T(1024)(128)(2,1)} %param.31) | copy-start | bytes 4612
  46.8 40.3 %copy-start.20 = (bf16[768]{0:T(1024)(128)(2,1)S(1)}, bf16[768]{0:T(1024)(128)(2,1)}, u32[]{:S(2)}) copy-start(bf16[768]{0:T(1024)(128)(2,1)} %param.35) | copy-start | bytes 4612
  46.8 40.9 %copy-start.21 = (bf16[768]{0:T(1024)(128)(2,1)S(1)}, bf16[768]{0:T(1024)(128)(2,1)}, u32[]{:S(2)}) copy-start(bf16[768]{0:T(1024)(128)(2,1)} %param.36) | copy-start | bytes 4612
  46.8 41.4 %copy-start.22 = (bf16[768]{0:T(1024)(128)(2,1)S(1)}, bf16[768]{0:T(1024)(128)(2,1)}, u32[]{:S(2)}) copy-start(bf16[768]{0:T(1024)(128)(2,1)} %param.37) | copy-start | bytes 4612
  46.9 403.2 %reduce-scatter.6.cloned.1.call-start = ((), (), s32[]{:S(2)}) async-start(), calls=%async_computation.6 | async-start | bytes 13762560 | tf_op jit(solution)/shard_map/reduce_scatter | solution.py:545
  46.9 0.7 collective-permute-start
  47.6 23.0 %copy-start.4 = (bf16[512,768]{1,0:T(8,128)(2,1)}, bf16[512,768]{1,0:T(8,128)(2,1)S(1)}, u32[]{:S(2)}) copy-start(bf16[512,768]{1,0:T(8,128)(2,1)S(1)} %collective-permute-done.hid_ref) | copy-start | bytes 2359300
  47.7 22.9 %collective-permute-start.1 = (bf16[512,768]{1,0:T(8,128)(2,1)S(1)}, bf16[512,768]{1,0:T(8,128)(2,1)S(1)}, u32[]{:S(2)}, u32[]{:S(2)}) collective-permute-start(bf16[512,768]{1,0:T(8,128)(2,1)S(1)} %collective-permute-done.hid_ref), channel_id=1, source_target_pairs={{0,4},{1,5},{2,6},{3,7},{4,0},{5,1},{6,2},{7,3},{8,12},{9,13},{10,... | collective-permute-start | bytes 2359304 | tf_op jit(solution)/shard_map/ppermute | solution.py:485
  70.6 1.4 copy-start.6
  72.0 64.4 %collective-permute-start.2 = (bf16[2,512,768]{2,1,0:T(8,128)(2,1)}, bf16[2,512,768]{2,1,0:T(8,128)(2,1)}, u32[]{:S(2)}, u32[]{:S(2)}) collective-permute-start(bf16[2,512,768]{2,1,0:T(8,128)(2,1)} %pad_maximum_fusion), channel_id=1, source_target_pairs={{0,1},{1,0},{2,3},{3,2},{4,5},{5,4},{6,7},{7,6},{8,9},{9,8},{10,11... | collective-permute-start | bytes 4718600 | tf_op jit(solution)/shard_map/ppermute | solution.py:485
  72.7 16.2 %collective-permute-start.4 = (s32[2049]{0:T(1024)S(1)}, s32[2049]{0:T(1024)S(1)}, u32[]{:S(2)}, u32[]{:S(2)}) collective-permute-start(s32[2049]{0:T(1024)S(1)} %constant_dynamic-update-slice_fusion), channel_id=1, source_target_pairs={{0,4},{4,0},{8,12},{12,8},{16,20},{20,16},{24,28},{28,24},{1,5},{5... | collective-permute-start | bytes 24596 | tf_op jit(solution)/shard_map/ppermute | solution.py:488
  73.1 107.9 %collective-permute-start.8 = (bf16[512,768]{1,0:T(8,128)(2,1)}, bf16[512,768]{1,0:T(8,128)(2,1)}, u32[]{:S(2)}, u32[]{:S(2)}) collective-permute-start(bf16[512,768]{1,0:T(8,128)(2,1)} %param.22), channel_id=1, source_target_pairs={{0,0},{1,1},{2,4},{3,5},{4,2},{5,3},{6,6},{7,7},{8,8},{9,9},{10,12... | collective-permute-start | bytes 2359304 | tf_op jit(solution)/shard_map/ppermute | solution.py:482
  81.7 57.2 %collective-permute-start.3 = (bf16[768,1152]{1,0:T(8,128)(2,1)}, bf16[768,1152]{1,0:T(8,128)(2,1)S(1)}, u32[]{:S(2)}, u32[]{:S(2)}) collective-permute-start(bf16[768,1152]{1,0:T(8,128)(2,1)} %all-gather.5.cloned.1.call-done), channel_id=1, source_target_pairs={{0,0},{1,1},{2,4},{3,5},{4,2},{5,3},{6,6},{7,7},{8,8},{9,9},{10,12... | collective-permute-start | bytes 5308424 | tf_op jit(solution)/shard_map/ppermute | solution.py:482
  88.9 1.4 copy-start.5
  90.3 47.3 %copy-start.7 = (bf16[512,768]{1,0:T(8,128)(2,1)S(1)}, bf16[512,768]{1,0:T(8,128)(2,1)}, u32[]{:S(2)}) copy-start(bf16[512,768]{1,0:T(8,128)(2,1)} %copy-done.6) | copy-start | bytes 2359300
  138.8 2.2 copy-start.3
  138.9 2.6 copy-start.23
  178.2 7.8 %collective-permute-start.5 = (bf16[1,192,512]{2,1,0:T(8,128)(2,1)S(1)}, bf16[1,192,512]{2,1,0:T(8,128)(2,1)S(1)}, u32[]{:S(2)}, u32[]{:S(2)}) collective-permute-start(bf16[1,192,512]{2,1,0:T(8,128)(2,1)S(1)} %get-tuple-element.121), channel_id=1, source_target_pairs={{0,1},{1,0},{2,3},{3,2},{4,5},{5,4},{6,7},{7,6},{8,9},{9,8},{10,11... | collective-permute-start | bytes 589832 | tf_op jit(solution)/shard_map/ppermute | solution.py:485
  178.2 7.8 %collective-permute-start.6 = (bf16[1,192,512]{2,1,0:T(8,128)(2,1)S(1)}, bf16[1,192,512]{2,1,0:T(8,128)(2,1)S(1)}, u32[]{:S(2)}, u32[]{:S(2)}) collective-permute-start(bf16[1,192,512]{2,1,0:T(8,128)(2,1)S(1)} %get-tuple-element.120), channel_id=1, source_target_pairs={{0,4},{1,5},{2,6},{3,7},{4,0},{5,1},{6,2},{7,3},{8,12},{9,13},{10,... | collective-permute-start | bytes 589832 | tf_op jit(solution)/shard_map/ppermute | solution.py:485
  178.2 9.1 %collective-permute-start.7 = (bf16[1,192,512]{2,1,0:T(8,128)(2,1)S(1)}, bf16[1,192,512]{2,1,0:T(8,128)(2,1)S(1)}, u32[]{:S(2)}, u32[]{:S(2)}) collective-permute-start(bf16[1,192,512]{2,1,0:T(8,128)(2,1)S(1)} %get-tuple-element.119), channel_id=1, source_target_pairs={{0,5},{1,4},{2,7},{3,6},{4,1},{5,0},{6,3},{7,2},{8,13},{9,12},{10,... | collective-permute-start | bytes 589832 | tf_op jit(solution)/shard_map/ppermute | solution.py:485
  186.0 2.1 copy-start.25
  186.0 2.1 copy-start.26
  228.4 1.1 copy-start.11
  228.4 304.4 %reduce-scatter.4.cloned.1.call-start = ((), (), s32[]{:S(2)}) async-start(), calls=%async_computation.5 | async-start | bytes 1990656 | tf_op jit(solution)/shard_map/reduce_scatter | solution.py:559
  229.6 7.5 %collective-permute-start.10 = (bf16[1,192,512]{2,1,0:T(8,128)(2,1)S(1)}, bf16[1,192,512]{2,1,0:T(8,128)(2,1)S(1)}, u32[]{:S(2)}, u32[]{:S(2)}) collective-permute-start(bf16[1,192,512]{2,1,0:T(8,128)(2,1)S(1)} %get-tuple-element.118), channel_id=1, source_target_pairs={{0,1},{1,0},{2,3},{3,2},{4,5},{5,4},{6,7},{7,6},{8,9},{9,8},{10,11... | collective-permute-start | bytes 589832 | tf_op jit(solution)/shard_map/ppermute | solution.py:485
  230.7 6.4 %collective-permute-start.11 = (bf16[1,192,512]{2,1,0:T(8,128)(2,1)S(1)}, bf16[1,192,512]{2,1,0:T(8,128)(2,1)S(1)}, u32[]{:S(2)}, u32[]{:S(2)}) collective-permute-start(bf16[1,192,512]{2,1,0:T(8,128)(2,1)S(1)} %get-tuple-element.117), channel_id=1, source_target_pairs={{0,4},{1,5},{2,6},{3,7},{4,0},{5,1},{6,2},{7,3},{8,12},{9,13},{10,... | collective-permute-start | bytes 589832 | tf_op jit(solution)/shard_map/ppermute | solution.py:485
  231.0 22.7 %collective-permute-start.12 = (bf16[1,192,512]{2,1,0:T(8,128)(2,1)S(1)}, bf16[1,192,512]{2,1,0:T(8,128)(2,1)S(1)}, u32[]{:S(2)}, u32[]{:S(2)}) collective-permute-start(bf16[1,192,512]{2,1,0:T(8,128)(2,1)S(1)} %get-tuple-element.116), channel_id=1, source_target_pairs={{0,5},{1,4},{2,7},{3,6},{4,1},{5,0},{6,3},{7,2},{8,13},{9,12},{10,... | collective-permute-start | bytes 589832 | tf_op jit(solution)/shard_map/ppermute | solution.py:485
  304.8 2.1 collective-permute-start.16
  306.9 1.2 copy-start.8
  308.1 235.3 %reduce-scatter.8.cloned.1.call-start = ((), (), s32[]{:S(2)}) async-start(), calls=%async_computation.7 | async-start | bytes 3096576 | tf_op jit(solution)/shard_map/reduce_scatter | solution.py:546
  316.6 136.9 %copy-start.2 = (bf16[4,512,768]{2,1,0:T(8,128)(2,1)S(1)}, bf16[4,512,768]{2,1,0:T(8,128)(2,1)}, u32[]{:S(2)}) copy-start(bf16[4,512,768]{2,1,0:T(8,128)(2,1)} %input_grad.1) | copy-start | bytes 9437188
  319.4 134.1 %collective-permute-start.13 = (bf16[2,512,768]{2,1,0:T(8,128)(2,1)}, bf16[2,512,768]{2,1,0:T(8,128)(2,1)}, u32[]{:S(2)}, u32[]{:S(2)}) collective-permute-start(bf16[2,512,768]{2,1,0:T(8,128)(2,1)} %slice.138), channel_id=1, source_target_pairs={{0,4},{1,5},{2,6},{3,7},{4,0},{5,1},{6,2},{7,3},{8,12},{9,13},{10,... | collective-permute-start | bytes 4718600 | tf_op jit(solution)/shard_map/ppermute | solution.py:485
  455.3 28.5 %copy-start.9 = (f32[512,768]{1,0:T(8,128)S(1)}, f32[512,768]{1,0:T(8,128)}, u32[]{:S(2)}) copy-start(f32[512,768]{1,0:T(8,128)} %get-tuple-element.42) | copy-start | bytes 4718596
  455.4 28.4 %collective-permute-start.14 = (bf16[512,768]{1,0:T(8,128)(2,1)S(1)}, bf16[512,768]{1,0:T(8,128)(2,1)S(1)}, u32[]{:S(2)}, u32[]{:S(2)}) collective-permute-start(bf16[512,768]{1,0:T(8,128)(2,1)S(1)} %fusion.3), channel_id=1, source_target_pairs={{0,1},{1,0},{2,3},{3,2},{4,5},{5,4},{6,7},{7,6},{8,9},{9,8},{10,11... | collective-permute-start | bytes 2359304 | tf_op jit(solution)/shard_map/ppermute | solution.py:485
  457.2 74.3 %collective-permute-start.9 = (bf16[512,768]{1,0:T(8,128)(2,1)}, bf16[512,768]{1,0:T(8,128)(2,1)S(1)}, u32[]{:S(2)}, u32[]{:S(2)}) collective-permute-start(bf16[512,768]{1,0:T(8,128)(2,1)} %get-tuple-element.41), channel_id=1, source_target_pairs={{0,0},{1,1},{2,4},{3,5},{4,2},{5,3},{6,6},{7,7},{8,8},{9,9},{10,12... | collective-permute-start | bytes 2359304 | tf_op jit(solution)/shard_map/ppermute | solution.py:482
  483.7 1.0 copy-start.16
  484.0 47.6 %collective-permute-start.15 = (bf16[512,768]{1,0:T(8,128)(2,1)S(1)}, bf16[512,768]{1,0:T(8,128)(2,1)S(1)}, u32[]{:S(2)}, u32[]{:S(2)}) collective-permute-start(bf16[512,768]{1,0:T(8,128)(2,1)S(1)} %fusion.2), channel_id=1, source_target_pairs={{0,0},{1,1},{2,4},{3,5},{4,2},{5,3},{6,6},{7,7},{8,8},{9,9},{10,12... | collective-permute-start | bytes 2359304 | tf_op jit(solution)/shard_map/ppermute | solution.py:482
  543.4 2.6 copy-start.10
  543.4 4.2 copy-start.1
  (3 other events, 2.9 us)
Sparse Core Ops, SparseCore 0:
  10.2 36.5 all-gather.8
  49.2 25.4 all-gather.4
  76.6 65.4 all-gather.6
  228.5 216.5 reduce-scatter.5
  448.4 46.8 reduce-scatter.3
  498.5 44.9 reduce-scatter.7
